TPU v7x, 128 devices: a whole 4x4x4 slice. The times are simulated.
128 devices in a mesh: section: 2 (over core), row: 32 (over z, y, x_hi), col: 2 (over x_lo).
Axes of the slice: x: 4 (x_hi: 2, x_lo: 2; x = x_hi * 2 + x_lo), y: 4, z: 4, core: 2. Of those that a mesh axis runs over, the one named last changes fastest.
Arguments:
- latents: bfloat16 [32, 4, 256, 1152], P('row', None, 'col'), may hold values from -6 to 6
- timesteps: int32 [32], P('row'), may hold values from 0 to 999
- lengths: int32 [32], P('row'), may hold values from 1 to 1024, 24576 in all
- patch_order: int32 [4], replicated, may hold values from 0 to 3, each once
- ada_weight: bfloat16 [2, 1152, 6, 1152], P('section', 'row', None, 'col'), may hold values from -0.1875 to 0.1875
- qkv_weight: bfloat16 [2, 1152, 3, 1152], P('section', 'row', None, 'col'), may hold values from -1 to 1
- out_weight: bfloat16 [2, 1152, 1152], P('section', 'col', 'row'), may hold values from -0.1875 to 0.1875
- up_weight: bfloat16 [2, 1152, 4608], P('section', 'row', 'col'), may hold values from -0.1875 to 0.1875
- down_weight: bfloat16 [2, 4608, 1152], P('section', 'col', 'row'), may hold values from -0.09375 to 0.09375
- stale_keys: bfloat16 [2, 32, 4, 256, 1152], P('section', 'row', None, None, 'col'), may hold values from -9 to 9
- stale_values: bfloat16 [2, 32, 4, 256, 1152], P('section', 'row', None, None, 'col'), may hold values from -6 to 6
Outputs:
- section_out: bfloat16 [2, 32, 4, 256, 1152], P('section', 'row', None, 'col')
Inputs may be any that keep to these rules, and one draw needn't show every extreme that they name: `lengths`: tokens that serve as keys in each request; some request has all 1024. `patch_order`: each of the 4 patches once.
All inputs are finite; a program needn't handle non-finite values. No bound on the sum of `lengths` on one device may be relied on, other than what follows from the above.
Results may differ from a plain program's by a relative error of at most 0.0095.
Values may be sent and summed in bfloat16 or wider, within the bound.
A program may use at most 128 MiB of HBM per device.

v0:
```python
import math

import jax
import jax.numpy as jnp
from jax import lax
from jax.sharding import PartitionSpec as P

D = 1152
HD = 72


def passed_along(shard, axis, by):
    size = lax.axis_size(axis)
    pairs = [(i, i + by) for i in range(size) if 0 <= i + by < size]
    return lax.ppermute(shard, axis, pairs)


def sinusoid(step_ids):
    half_width = D // 2
    frequency = jnp.exp(-math.log(10000.0) * jnp.arange(half_width, dtype=jnp.float32) / half_width)
    angles = step_ids.astype(jnp.float32)[:, None] * frequency[None, :]
    return jnp.concatenate([jnp.cos(angles), jnp.sin(angles)], axis=1)


def layer_norm(inputs):
    center = jnp.mean(inputs, axis=-1, keepdims=True)
    spread = jnp.mean(jnp.square(inputs - center), axis=-1, keepdims=True)
    return (inputs - center) * lax.rsqrt(spread + 1e-06)


def attend(queries, keys, values, valid_keys):
    scores = jnp.einsum(
        "bqhd,bkhd->bhqk", queries, keys, preferred_element_type=jnp.float32
    ) / math.sqrt(HD)
    scores = jnp.where(valid_keys[:, None, None, :], scores, -1e30)
    top_score = jnp.max(scores, axis=-1, keepdims=True)
    weights = jnp.exp(scores - top_score)
    totals = jnp.sum(weights, axis=-1)
    probs = weights.astype(jnp.bfloat16)
    mixed = jnp.einsum("bhqk,bkhd->bqhd", probs, values, preferred_element_type=jnp.float32)
    return (mixed / jnp.transpose(totals, (0, 2, 1))[..., None]).astype(jnp.bfloat16)


def put_slot(buffer, new_slot, patch_id, active):
    old_slot = lax.dynamic_index_in_dim(buffer, patch_id, 1, keepdims=False)
    return lax.dynamic_update_index_in_dim(
        buffer, jnp.where(active, new_slot, old_slot), patch_id, 1
    )


def local(
    latents,
    timesteps,
    lengths,
    patch_order,
    ada_weight,
    qkv_weight,
    out_weight,
    up_weight,
    down_weight,
    stale_keys,
    stale_values,
):
    section_id = lax.axis_index("section")
    ada_local = ada_weight[0]
    qkv_local = qkv_weight[0]
    up_local = up_weight[0]
    qkv_full, up_full, ada_full = (
        lax.all_gather(qkv_local, "row", axis=0, tiled=True),
        lax.all_gather(up_local, "row", axis=0, tiled=True),
        lax.all_gather(ada_local, "row", axis=0, tiled=True),
    )
    cond = jax.nn.silu(sinusoid(timesteps)).astype(jnp.bfloat16)
    mod_cols = jnp.einsum("rd,dkc->rkc", cond, ada_full, preferred_element_type=jnp.float32)
    out_full, down_full = (
        lax.all_gather(out_weight[0], "row", axis=1, tiled=True),
        lax.all_gather(down_weight[0], "row", axis=1, tiled=True),
    )
    modulation = lax.all_gather(mod_cols, "col", axis=2, tiled=True)
    shift_attn = modulation[:, 0][:, None, :]
    scale_attn = modulation[:, 1][:, None, :]
    gate_attn = modulation[:, 2][:, None, :]
    shift_mlp = modulation[:, 3][:, None, :]
    scale_mlp = modulation[:, 4][:, None, :]
    gate_mlp = modulation[:, 5][:, None, :]
    key_buffer = stale_keys[0]
    value_buffer = stale_values[0]
    req_local, patch_count, patch_tokens, head_cols = key_buffer.shape
    heads_local = head_cols // HD
    seq_len = patch_count * patch_tokens
    valid_keys = jnp.arange(seq_len, dtype=jnp.int32)[None, :] < lengths[:, None]
    local_tokens = latents.shape[2]
    width_full = latents.shape[3]
    results = jnp.zeros((req_local, patch_count, local_tokens, width_full), jnp.bfloat16)
    previous = jnp.zeros((req_local, local_tokens, width_full), jnp.bfloat16)
    for tick_index in range(patch_count + 1):
        position = tick_index - section_id
        active = (position >= 0) & (position < patch_count)
        patch_id = patch_order[jnp.clip(position, 0, patch_count - 1)]
        own_tokens = lax.dynamic_index_in_dim(latents, patch_id, 1, keepdims=False)
        if tick_index > 0:
            arrived = passed_along(previous, "section", 1)
            current = jnp.where(section_id == 0, own_tokens, arrived)
        else:
            current = own_tokens
        tokens_in = current.astype(jnp.float32)
        normed = (layer_norm(tokens_in) * (1.0 + scale_attn) + shift_attn).astype(jnp.bfloat16)
        whole = lax.all_gather(normed, "col", axis=1, tiled=True)
        projected = jnp.einsum(
            "rtd,dkc->rtkc", whole, qkv_full, preferred_element_type=jnp.float32
        ).astype(jnp.bfloat16)
        key_buffer = put_slot(key_buffer, projected[:, :, 1], patch_id, active)
        value_buffer = put_slot(value_buffer, projected[:, :, 2], patch_id, active)
        attended = attend(
            projected[:, :, 0].reshape(req_local, patch_tokens, heads_local, HD),
            key_buffer.reshape(req_local, seq_len, heads_local, HD),
            value_buffer.reshape(req_local, seq_len, heads_local, HD),
            valid_keys,
        ).reshape(req_local, patch_tokens, head_cols)
        attn_partial = jnp.einsum(
            "rtc,cd->rtd", attended, out_full, preferred_element_type=jnp.float32
        )
        attn_summed = lax.psum_scatter(
            attn_partial.astype(jnp.bfloat16), "col", scatter_dimension=1, tiled=True
        ).astype(jnp.float32)
        after_attn = tokens_in + gate_attn * attn_summed
        normed_mlp = (layer_norm(after_attn) * (1.0 + scale_mlp) + shift_mlp).astype(jnp.bfloat16)
        whole_mlp = lax.all_gather(normed_mlp, "col", axis=1, tiled=True)
        hidden = jax.nn.gelu(
            jnp.einsum("rtd,df->rtf", whole_mlp, up_full, preferred_element_type=jnp.float32),
            approximate=True,
        ).astype(jnp.bfloat16)
        mlp_partial = jnp.einsum(
            "rtf,fd->rtd", hidden, down_full, preferred_element_type=jnp.float32
        )
        mlp_summed = lax.psum_scatter(
            mlp_partial.astype(jnp.bfloat16), "col", scatter_dimension=1, tiled=True
        ).astype(jnp.float32)
        result = (after_attn + gate_mlp * mlp_summed).astype(jnp.bfloat16)
        results = put_slot(results, result, patch_id, active)
        previous = result
    return results[None]


def solution(mesh):
    return jax.shard_map(
        local,
        mesh=mesh,
        in_specs=(
            P("row", None, "col", None),
            P("row"),
            P("row"),
            P(),
            P("section", "row", None, "col"),
            P("section", "row", None, "col"),
            P("section", "col", "row"),
            P("section", "row", "col"),
            P("section", "col", "row"),
            P("section", "row", None, None, "col"),
            P("section", "row", None, None, "col"),
        ),
        out_specs=P("section", "row", None, "col", None),
        check_vma=False,
    )
```

profile of v0, /device:TPU:1, one launch (start us, length us, event | category | flops | bytes accessed | tf_op | source)
XLA Modules:
  0.0 1007.3 jit_solution(821713354570099396)
XLA Ops:
  22.2 64.5 %all-gather.17.cloned.1.call-done = bf16[1,576,1152]{1,0,2:T(2,128)(2,1)} async-done(((bf16[1,576,36]{1,0,2:T(2,128)(2,1)}), bf16[1,576,1152]{1,0,2:T(2,128)(2,1)}) %all-gather.17.cloned.1.call-update) | async-done | bytes 1327120 | tf_op jit(solution)/shard_map/all_gather | solution.py:76
  86.7 6.7 copy.48
  93.4 85.9 %all-gather.15.cloned.1.call-done = bf16[1,1152,3,576]{3,2,0,1:T(4,128)(2,1)} async-done(((bf16[1,36,3,576]{3,2,0,1:T(4,128)(2,1)}), bf16[1,1152,3,576]{3,2,0,1:T(4,128)(2,1)}) %all-gather.15.cloned.1.call-update) | async-done | bytes 3981328 | tf_op jit(solution)/shard_map/all_gather | solution.py:69
  179.3 11.3 %copy.44 = bf16[1,1152,3,576]{1,3,2,0:T(8,128)(2,1)} copy(bf16[1,1152,3,576]{3,2,0,1:T(4,128)(2,1)} %all-gather.15.cloned.1.call-done) | data formatting | bytes 7962624 | tf_op jit(solution)/shard_map/all_gather | solution.py:69
  190.6 115.0 %all-gather.13.cloned.1.call-done = bf16[1,1152,6,576]{3,2,0,1:T(8,128)(2,1)} async-done(((bf16[1,36,6,576]{3,2,0,1:T(8,128)(2,1)}), bf16[1,1152,6,576]{3,2,0,1:T(8,128)(2,1)}) %all-gather.13.cloned.1.call-update) | async-done | bytes 7962640 | tf_op jit(solution)/shard_map/all_gather | solution.py:71
  305.7 6.6 fusion
  320.3 7.6 all_gather.50
  327.8 3.5 fusion.189
  335.2 3.4 reshape.837
  352.7 72.8 %all-gather.21.cloned.1.call-done = bf16[1,2304,1152]{1,0,2:T(2,128)(2,1)} async-done(((bf16[1,2304,36]{1,0,2:T(2,128)(2,1)}), bf16[1,2304,1152]{1,0,2:T(2,128)(2,1)}) %all-gather.21.cloned.1.call-update) | async-done | bytes 5308432 | tf_op jit(solution)/shard_map/all_gather | solution.py:77
  425.5 23.4 %copy.51 = bf16[1,2304,1152]{2,1,0:T(8,128)(2,1)} copy(bf16[1,2304,1152]{1,0,2:T(2,128)(2,1)} %all-gather.21.cloned.1.call-done) | data formatting | bytes 10616832 | tf_op jit(solution)/shard_map/all_gather | solution.py:77
  448.8 95.5 %all-gather.19.cloned.1.call-done = bf16[1,1152,2304]{2,0,1:T(2,128)(2,1)} async-done(((bf16[1,36,2304]{2,0,1:T(2,128)(2,1)}), bf16[1,1152,2304]{2,0,1:T(2,128)(2,1)}) %all-gather.19.cloned.1.call-update) | async-done | bytes 5308432 | tf_op jit(solution)/shard_map/all_gather | solution.py:70
  544.3 7.2 copy.62
  551.5 11.2 %reduce-scatter.11.cloned.1.call-done = bf16[1,128,1152]{2,1,0:T(8,128)(2,1)} async-done(((bf16[1,256,1152]{2,1,0:T(8,128)(2,1)}), bf16[1,128,1152]{2,1,0:T(8,128)(2,1)}) %reduce-scatter.11.cloned.1.call-update) | async-done | bytes 294928 | tf_op jit(solution)/shard_map/reduce_scatter | solution.py:123
  566.2 8.8 all_gather.53
  575.0 8.3 fusion.89
  583.4 19.8 %reduce-scatter.13.cloned.1.call-done = bf16[1,128,1152]{2,1,0:T(8,128)(2,1)} async-done(((bf16[1,256,1152]{2,1,0:T(8,128)(2,1)}), bf16[1,128,1152]{2,1,0:T(8,128)(2,1)}) %reduce-scatter.13.cloned.1.call-update) | async-done | bytes 294928 | tf_op jit(solution)/shard_map/reduce_scatter | solution.py:136
  612.4 8.4 all_gather.56
  620.8 3.5 fusion.186
  626.4 3.4 reshape.843
  631.7 3.4 reshape.841
  643.8 19.9 %reduce-scatter.15.cloned.1.call-done = bf16[1,128,1152]{2,1,0:T(8,128)(2,1)} async-done(((bf16[1,256,1152]{2,1,0:T(8,128)(2,1)}), bf16[1,128,1152]{2,1,0:T(8,128)(2,1)}) %reduce-scatter.15.cloned.1.call-update) | async-done | bytes 294928 | tf_op jit(solution)/shard_map/reduce_scatter | solution.py:123
  667.2 9.0 all_gather.57
  676.1 8.2 fusion.86
  685.4 18.7 %reduce-scatter.17.cloned.1.call-done = bf16[1,128,1152]{2,1,0:T(8,128)(2,1)} async-done(((bf16[1,256,1152]{2,1,0:T(8,128)(2,1)}), bf16[1,128,1152]{2,1,0:T(8,128)(2,1)}) %reduce-scatter.17.cloned.1.call-update) | async-done | bytes 294928 | tf_op jit(solution)/shard_map/reduce_scatter | solution.py:136
  711.4 8.7 all_gather.58
  720.1 3.5 fusion.183
  725.6 3.4 reshape.849
  730.9 3.4 reshape.847
  743.0 19.7 %reduce-scatter.19.cloned.1.call-done = bf16[1,128,1152]{2,1,0:T(8,128)(2,1)} async-done(((bf16[1,256,1152]{2,1,0:T(8,128)(2,1)}), bf16[1,128,1152]{2,1,0:T(8,128)(2,1)}) %reduce-scatter.19.cloned.1.call-update) | async-done | bytes 294928 | tf_op jit(solution)/shard_map/reduce_scatter | solution.py:123
  766.2 8.7 all_gather.59
  774.9 8.2 fusion.83
  784.2 18.7 %reduce-scatter.21.cloned.1.call-done = bf16[1,128,1152]{2,1,0:T(8,128)(2,1)} async-done(((bf16[1,256,1152]{2,1,0:T(8,128)(2,1)}), bf16[1,128,1152]{2,1,0:T(8,128)(2,1)}) %reduce-scatter.21.cloned.1.call-update) | async-done | bytes 294928 | tf_op jit(solution)/shard_map/reduce_scatter | solution.py:136
  810.2 8.6 all_gather.60
  818.8 3.5 fusion.180
  824.3 3.4 reshape.855
  829.7 3.4 reshape.853
  841.7 19.7 %reduce-scatter.23.cloned.1.call-done = bf16[1,128,1152]{2,1,0:T(8,128)(2,1)} async-done(((bf16[1,256,1152]{2,1,0:T(8,128)(2,1)}), bf16[1,128,1152]{2,1,0:T(8,128)(2,1)}) %reduce-scatter.23.cloned.1.call-update) | async-done | bytes 294928 | tf_op jit(solution)/shard_map/reduce_scatter | solution.py:123
  865.0 8.8 all_gather.61
  873.7 8.2 fusion.80
  883.0 18.8 %reduce-scatter.25.cloned.1.call-done = bf16[1,128,1152]{2,1,0:T(8,128)(2,1)} async-done(((bf16[1,256,1152]{2,1,0:T(8,128)(2,1)}), bf16[1,128,1152]{2,1,0:T(8,128)(2,1)}) %reduce-scatter.25.cloned.1.call-update) | async-done | bytes 294928 | tf_op jit(solution)/shard_map/reduce_scatter | solution.py:136
  909.1 8.4 all_gather.62
  917.5 3.5 fusion.177
  927.6 3.4 reshape.859
  938.4 19.9 %reduce-scatter.27.cloned.1.call-done = bf16[1,128,1152]{2,1,0:T(8,128)(2,1)} async-done(((bf16[1,256,1152]{2,1,0:T(8,128)(2,1)}), bf16[1,128,1152]{2,1,0:T(8,128)(2,1)}) %reduce-scatter.27.cloned.1.call-update) | async-done | bytes 294928 | tf_op jit(solution)/shard_map/reduce_scatter | solution.py:123
  961.8 8.8 all_gather.63
  970.6 8.2 fusion.77
  981.2 17.4 %reduce-scatter.29.cloned.1.call-done = bf16[1,128,1152]{2,1,0:T(8,128)(2,1)} async-done(((bf16[1,256,1152]{2,1,0:T(8,128)(2,1)}), bf16[1,128,1152]{2,1,0:T(8,128)(2,1)}) %reduce-scatter.29.cloned.1.call-update) | async-done | bytes 294928 | tf_op jit(solution)/shard_map/reduce_scatter | solution.py:136
  (249 shorter events, 138.5 us)
Async XLA Ops:
  6.5 7.2 copy-start.36
  6.5 8.3 copy-start.42
  6.5 11.0 %copy-start.5 = (bf16[1,1,4,256,576]{3,4,2,1,0:T(8,128)(2,1)S(1)}, bf16[1,1,4,256,576]{3,4,2,1,0:T(8,128)(2,1)}, u32[]{:S(2)}) copy-start(bf16[1,1,4,256,576]{3,4,2,1,0:T(8,128)(2,1)} %param.20) | copy-start | bytes 3538948
  6.5 80.2 %all-gather.17.cloned.1.call-start = ((), (), s32[]{:S(2)}) async-start(), calls=%async_computation.22 | async-start | bytes 3041280 | tf_op jit(solution)/shard_map/all_gather | solution.py:76
  8.2 171.1 %all-gather.15.cloned.1.call-start = ((), (), s32[]{:S(2)}) async-start(), calls=%async_computation.21 | async-start | bytes 6082560 | tf_op jit(solution)/shard_map/all_gather | solution.py:69
  9.9 295.8 %all-gather.13.cloned.1.call-start = ((), (), s32[]{:S(2)}) async-start(), calls=%async_computation.20 | async-start | bytes 12165120 | tf_op jit(solution)/shard_map/all_gather | solution.py:71
  11.7 413.8 %all-gather.21.cloned.1.call-start = ((), (), s32[]{:S(2)}) async-start(), calls=%async_computation.24 | async-start | bytes 10948608 | tf_op jit(solution)/shard_map/all_gather | solution.py:77
  13.7 530.6 %all-gather.19.cloned.1.call-start = ((), (), s32[]{:S(2)}) async-start(), calls=%async_computation.23 | async-start | bytes 10948608 | tf_op jit(solution)/shard_map/all_gather | solution.py:70
  14.8 547.9 %reduce-scatter.11.cloned.1.call-start = ((), (), s32[]{:S(2)}) async-start(), calls=%async_computation.10 | async-start | bytes 884736 | tf_op jit(solution)/shard_map/reduce_scatter | solution.py:123
  352.6 250.6 %reduce-scatter.13.cloned.1.call-start = ((), (), s32[]{:S(2)}) async-start(), calls=%async_computation.11 | async-start | bytes 884736 | tf_op jit(solution)/shard_map/reduce_scatter | solution.py:136
  583.4 80.3 %reduce-scatter.15.cloned.1.call-start = ((), (), s32[]{:S(2)}) async-start(), calls=%async_computation.12 | async-start | bytes 884736 | tf_op jit(solution)/shard_map/reduce_scatter | solution.py:123
  606.4 3.7 collective-permute-start
  629.8 5.3 slice-start.1
  629.8 5.3 copy-start.38
  642.2 23.8 %copy-start.20 = (f32[1152]{0:T(1024)S(1)}, f32[1152]{0:T(1024)}, u32[]{:S(2)}) copy-start(f32[1152]{0:T(1024)} %get-tuple-element.6) | copy-start | bytes 13828
  642.2 23.8 %copy-start.24 = (f32[1152]{0:T(1024)S(1)}, f32[1152]{0:T(1024)}, u32[]{:S(2)}) copy-start(f32[1152]{0:T(1024)} %get-tuple-element.7) | copy-start | bytes 13828
  643.7 60.4 %reduce-scatter.17.cloned.1.call-start = ((), (), s32[]{:S(2)}) async-start(), calls=%async_computation.13 | async-start | bytes 884736 | tf_op jit(solution)/shard_map/reduce_scatter | solution.py:136
  676.1 28.0 %copy-start.2 = (bf16[1,128,1152]{2,1,0:T(8,128)(2,1)S(1)}, bf16[1,128,1152]{2,1,0:T(8,128)(2,1)}, u32[]{:S(2)}) copy-start(bf16[1,128,1152]{2,1,0:T(8,128)(2,1)} %reduce-scatter.15.cloned.1.call-done) | copy-start | bytes 884740
  684.3 26.8 %copy-start.29 = (f32[1152]{0:T(1024)S(1)}, f32[1152]{0:T(1024)}, u32[]{:S(2)}) copy-start(f32[1152]{0:T(1024)} %copy-done.28) | copy-start | bytes 13828
  684.3 26.8 %copy-start.33 = (f32[1152]{0:T(1024)S(1)}, f32[1152]{0:T(1024)}, u32[]{:S(2)}) copy-start(f32[1152]{0:T(1024)} %copy-done.32) | copy-start | bytes 13828
  684.4 78.3 %reduce-scatter.19.cloned.1.call-start = ((), (), s32[]{:S(2)}) async-start(), calls=%async_computation.14 | async-start | bytes 884736 | tf_op jit(solution)/shard_map/reduce_scatter | solution.py:123
  706.1 3.7 collective-permute-start.1
  729.0 5.3 slice-start.2
  729.0 5.3 copy-start.39
  741.4 23.6 %copy-start.21 = (f32[1152]{0:T(1024)S(1)}, f32[1152]{0:T(1024)}, u32[]{:S(2)}) copy-start(f32[1152]{0:T(1024)} %get-tuple-element.6) | copy-start | bytes 13828
  741.4 23.6 %copy-start.25 = (f32[1152]{0:T(1024)S(1)}, f32[1152]{0:T(1024)}, u32[]{:S(2)}) copy-start(f32[1152]{0:T(1024)} %get-tuple-element.7) | copy-start | bytes 13828
  743.0 59.9 %reduce-scatter.21.cloned.1.call-start = ((), (), s32[]{:S(2)}) async-start(), calls=%async_computation.15 | async-start | bytes 884736 | tf_op jit(solution)/shard_map/reduce_scatter | solution.py:136
  774.9 28.0 %copy-start.3 = (bf16[1,128,1152]{2,1,0:T(8,128)(2,1)S(1)}, bf16[1,128,1152]{2,1,0:T(8,128)(2,1)}, u32[]{:S(2)}) copy-start(bf16[1,128,1152]{2,1,0:T(8,128)(2,1)} %reduce-scatter.19.cloned.1.call-done) | copy-start | bytes 884740
  783.1 26.8 %copy-start.30 = (f32[1152]{0:T(1024)S(1)}, f32[1152]{0:T(1024)}, u32[]{:S(2)}) copy-start(f32[1152]{0:T(1024)} %copy-done.28) | copy-start | bytes 13828
  783.1 26.8 %copy-start.34 = (f32[1152]{0:T(1024)S(1)}, f32[1152]{0:T(1024)}, u32[]{:S(2)}) copy-start(f32[1152]{0:T(1024)} %copy-done.32) | copy-start | bytes 13828
  783.2 78.3 %reduce-scatter.23.cloned.1.call-start = ((), (), s32[]{:S(2)}) async-start(), calls=%async_computation.16 | async-start | bytes 884736 | tf_op jit(solution)/shard_map/reduce_scatter | solution.py:123
  804.9 3.7 collective-permute-start.2
  827.7 5.3 slice-start.3
  827.7 5.3 copy-start.40
  840.1 23.7 %copy-start.22 = (f32[1152]{0:T(1024)S(1)}, f32[1152]{0:T(1024)}, u32[]{:S(2)}) copy-start(f32[1152]{0:T(1024)} %get-tuple-element.6) | copy-start | bytes 13828
  840.1 23.7 %copy-start.26 = (f32[1152]{0:T(1024)S(1)}, f32[1152]{0:T(1024)}, u32[]{:S(2)}) copy-start(f32[1152]{0:T(1024)} %get-tuple-element.7) | copy-start | bytes 13828
  841.7 60.1 %reduce-scatter.25.cloned.1.call-start = ((), (), s32[]{:S(2)}) async-start(), calls=%async_computation.17 | async-start | bytes 884736 | tf_op jit(solution)/shard_map/reduce_scatter | solution.py:136
  873.7 28.1 %copy-start.4 = (bf16[1,128,1152]{2,1,0:T(8,128)(2,1)S(1)}, bf16[1,128,1152]{2,1,0:T(8,128)(2,1)}, u32[]{:S(2)}) copy-start(bf16[1,128,1152]{2,1,0:T(8,128)(2,1)} %reduce-scatter.23.cloned.1.call-done) | copy-start | bytes 884740
  881.9 26.9 %copy-start.31 = (f32[1152]{0:T(1024)S(1)}, f32[1152]{0:T(1024)}, u32[]{:S(2)}) copy-start(f32[1152]{0:T(1024)} %copy-done.28) | copy-start | bytes 13828
  881.9 26.9 %copy-start.35 = (f32[1152]{0:T(1024)S(1)}, f32[1152]{0:T(1024)}, u32[]{:S(2)}) copy-start(f32[1152]{0:T(1024)} %copy-done.32) | copy-start | bytes 13828
  882.0 76.3 %reduce-scatter.27.cloned.1.call-start = ((), (), s32[]{:S(2)}) async-start(), calls=%async_computation.18 | async-start | bytes 884736 | tf_op jit(solution)/shard_map/reduce_scatter | solution.py:123
  903.8 3.7 collective-permute-start.3
  925.7 5.3 slice-start
  925.7 5.3 copy-start.41
  936.8 23.8 %copy-start.23 = (f32[1152]{0:T(1024)S(1)}, f32[1152]{0:T(1024)}, u32[]{:S(2)}) copy-start(f32[1152]{0:T(1024)} %get-tuple-element.6) | copy-start | bytes 13828
  936.8 23.8 %copy-start.27 = (f32[1152]{0:T(1024)S(1)}, f32[1152]{0:T(1024)}, u32[]{:S(2)}) copy-start(f32[1152]{0:T(1024)} %get-tuple-element.7) | copy-start | bytes 13828
  938.4 60.2 %reduce-scatter.29.cloned.1.call-start = ((), (), s32[]{:S(2)}) async-start(), calls=%async_computation.19 | async-start | bytes 884736 | tf_op jit(solution)/shard_map/reduce_scatter | solution.py:136
  978.8 19.8 %copy-start.1 = (bf16[1,128,1152]{2,1,0:T(8,128)(2,1)S(1)}, bf16[1,128,1152]{2,1,0:T(8,128)(2,1)}, u32[]{:S(2)}) copy-start(bf16[1,128,1152]{2,1,0:T(8,128)(2,1)} %reduce-scatter.27.cloned.1.call-done) | copy-start | bytes 884740
  (19 other events, 37.9 us)
Sparse Core Ops, SparseCore 0:
  10.5 76.1 all-gather.16
  89.7 89.5 all-gather.14
  182.3 123.2 all-gather.12
  308.5 116.9 all-gather.20
  428.4 115.8 all-gather.18
  546.5 16.1 reduce-scatter.10
  583.5 19.6 reduce-scatter.12
  643.8 19.7 reduce-scatter.14
  684.5 19.5 reduce-scatter.16
  743.1 19.5 reduce-scatter.18
  783.3 19.5 reduce-scatter.20
  841.8 19.5 reduce-scatter.22
  882.1 19.6 reduce-scatter.24
  938.5 19.7 reduce-scatter.26
  978.9 19.6 reduce-scatter.28
where the time goes:
time: 1010 us
  waiting for transfers between devices  619 us (61%)
  local copies, waits for them, and re-layouts  121 us (12%)
  matrix products  96.2 us (10%)
  blocking collectives  89 us (9%)
  other arithmetic  51 us (5%)
  between operations  25.1 us (2%)
    all_gather x1, waiting for transfers between devices, local(): lax.all_gather(ada_local, 'row', axis=0, tiled=True)  115 us
    all_gather x1, waiting for transfers between devices, local(): lax.all_gather(up_local, 'row', axis=0, tiled=True)  95.5 us
    reduce_scatter x5, waiting for transfers between devices, local(): lax.psum_scatter(mlp_partial.astype(jnp.bfloat16), 'col', scatter_dimensi...  93.3 us
    reduce_scatter x5, waiting for transfers between devices, local(): lax.psum_scatter(attn_partial.astype(jnp.bfloat16), 'col', scatter_dimens...  90.3 us
    all_gather x1, waiting for transfers between devices, local(): lax.all_gather(qkv_local, 'row', axis=0, tiled=True)  85.9 us
    all_gather x1, waiting for transfers between devices, local(): lax.all_gather(down_weight[0], 'row', axis=1, tiled=True)  72.8 us
    all_gather x1, waiting for transfers between devices, local(): lax.all_gather(out_weight[0], 'row', axis=1, tiled=True)  64.5 us
    all_gather x5, blocking collectives, local(): whole_mlp = lax.all_gather(normed_mlp, 'col', axis=1, tiled=True)  44.1 us
  transfers between devices with their start and end apart: 19, of which 19 were waited for; matrix products, arithmetic and copies ran while one was open for 10% of the time, Pallas kernels for 0%

commit v1 on v0

v1 whole, which is shorter than its diff:
```python
import math

import jax
import jax.numpy as jnp
from jax import lax
from jax.experimental import pallas as pl
from jax.experimental.pallas import tpu as pltpu
from jax.sharding import PartitionSpec as P

D = 1152
HD = 72
F32 = jnp.float32
BF16 = jnp.bfloat16

HEADW = 640
COL_OUT = 3 * HEADW
COL_UP = 4 * HEADW
COL_DOWN = COL_UP + 2304
COLS = COL_DOWN + 2304
QUARTER = COLS // 4
CHUNKS = ((0, COL_UP), (COL_UP, COL_DOWN), (COL_DOWN, COLS))
MAIN = 1024
MESH = pl.DeviceIdType.MESH
NT = (((1,), (1,)), ((), ()))


def sinusoid(step_ids):
    half_width = D // 2
    frequency = jnp.exp(-math.log(10000.0) * jnp.arange(half_width, dtype=F32) / half_width)
    angles = step_ids.astype(F32)[:, None] * frequency[None, :]
    return jnp.concatenate([jnp.cos(angles), jnp.sin(angles)], axis=1)


def halves(chunk):
    start, stop = CHUNKS[chunk]
    middle = start + (stop - start) // 2
    return ((start, middle - start), (middle, stop - middle))


def relay(
    valid_ref, mod_ref, lat_ref, stale_k, stale_v, main_ref, rem_ref, out_ref,
    wall, stag, wrem, x, x1, qs, kbuf, vbuf, att, hid, h, pa_own, pa_got, pm_own, pm_got, y,
    local_sem, xh_send, xh_recv, send_sem, recv_sem, col_send, col_recv, pass_send, pass_recv,
):
    sec = lax.axis_index("section")
    row = lax.axis_index("row")
    col = lax.axis_index("col")
    z, yy, xh = row // 8, lax.rem(row // 2, 4), lax.rem(row, 2)

    def at(section=None, zz=None, y_=None, x_=None, c=None):
        s_ = sec if section is None else section
        r_ = ((z if zz is None else zz) * 4 + (yy if y_ is None else y_)) * 2 + (xh if x_ is None else x_)
        return (s_, r_, col if c is None else c)

    y_peer = [lax.rem(yy + d, 4) for d in range(4)]
    z_peer = [lax.rem(z + d, 4) for d in range(4)]
    xh_dev = at(x_=1 - xh)
    col_dev = at(c=1 - col)
    sec_dev = at(section=1 - sec)

    barrier = pltpu.get_barrier_semaphore()
    for dev in (
        [xh_dev, col_dev, sec_dev]
        + [at(y_=y_peer[d]) for d in (1, 2, 3)]
        + [at(zz=z_peer[d]) for d in (1, 2, 3)]
    ):
        pl.semaphore_signal(barrier, inc=1, device_id=dev, device_id_type=MESH)
    pl.semaphore_wait(barrier, 9)

    def rdma(src, dst, s_sem, r_sem, dev):
        return pltpu.make_async_remote_copy(
            src_ref=src, dst_ref=dst, send_sem=s_sem, recv_sem=r_sem, device_id=dev, device_id_type=MESH
        )

    def buf(k):
        return (stag, 16, rem_ref) if k == 0 else (wall, 32, main_ref)

    def span(k, half):
        if k == 0:
            return ((0, QUARTER // 2), (QUARTER // 2, QUARTER // 2))[half]
        return halves(k - 1)[half]

    pieces = range(1 + len(CHUNKS))

    def xh_copy(k):
        ref, rows, src = buf(k)
        c0 = span(k, 0)[0]
        width = span(k, 0)[1] + span(k, 1)[1]
        return rdma(
            src.at[:, pl.ds(c0, width)],
            ref.at[z, yy, pl.ds(xh * rows, rows), pl.ds(c0, width)],
            xh_send.at[k], xh_recv.at[k], xh_dev,
        )

    def xh_arrival(k):
        ref, rows, src = buf(k)
        c0 = span(k, 0)[0]
        width = span(k, 0)[1] + span(k, 1)[1]
        return rdma(
            src.at[:, pl.ds(c0, width)],
            ref.at[z, yy, pl.ds((1 - xh) * rows, rows), pl.ds(c0, width)],
            xh_send.at[k], xh_recv.at[k], xh_dev,
        )

    def block(k, half, phase, zz, y_):
        ref = buf(k)[0]
        c0, width = span(k, half)
        if phase == 0:
            return ref.at[zz, y_, :, pl.ds(c0, width)]
        if half == 0:
            return ref.at[zz, :, :, pl.ds(c0, width)]
        return ref.at[:, y_, :, pl.ds(c0, width)]

    def ring_copy(k, half, phase, d, arrival):
        i = ((phase * 2 + half) * 4 + k) * 3 + d - 1
        along_y = (half == 0) == (phase == 0)
        if along_y:
            dev = at(y_=y_peer[d])
        else:
            dev = at(zz=z_peer[d])
        zz, y_ = z, yy
        if arrival:
            if along_y:
                y_ = y_peer[4 - d]
            else:
                zz = z_peer[4 - d]
        ref = block(k, half, phase, zz, y_)
        return rdma(ref, ref, send_sem.at[i], recv_sem.at[i], dev)

    own_main = pltpu.make_async_copy(main_ref, wall.at[z, yy, pl.ds(xh * 32, 32)], local_sem.at[0])
    own_rem = pltpu.make_async_copy(rem_ref, stag.at[z, yy, pl.ds(xh * 16, 16)], local_sem.at[1])
    own_main.start()
    own_rem.start()
    for k in pieces:
        xh_copy(k).start()

    x_mine = x.at[:, pl.ds(col * 128, 128)]

    @pl.when(sec == 0)
    def _():
        rdma(lat_ref, x_mine, pass_send.at[4], pass_recv.at[4], col_dev).start()
        x[:, pl.ds(col * 128, 128), :] = lat_ref[...]

    kbuf[...] = stale_k[...]
    vbuf[...] = stale_v[...]
    att[...] = jnp.zeros_like(att)

    own_main.wait()
    own_rem.wait()
    for k in pieces:
        xh_arrival(k).wait_recv()
        for half in (0, 1):
            for d in (1, 3, 2):
                ring_copy(k, half, 0, d, False).start()
    for k in pieces:
        for half in (0, 1):
            for d in (1, 2, 3):
                ring_copy(k, half, 0, d, True).wait_recv()
            for d in (1, 3, 2):
                ring_copy(k, half, 1, d, False).start()

    def arrived(k):
        for half in (0, 1):
            for d in (1, 2, 3):
                ring_copy(k, half, 1, d, True).wait_recv()

    arrived(0)
    rows_i = lax.broadcasted_iota(jnp.int32, (128, 512), 0)
    cols_i = lax.broadcasted_iota(jnp.int32, (128, 512), 1)
    for q in range(4):
        pick = jnp.where(
            ((cols_i >> 4) == (rows_i >> 2)) & ((cols_i & 15) == 4 * q + (rows_i & 3)), 1.0, 0.0
        ).astype(BF16)
        for n in range(QUARTER // 256):
            part = stag[:, :, :, n * 256:(n + 1) * 256].reshape(512, 256)
            wrem[:, q * QUARTER + n * 256:q * QUARTER + (n + 1) * 256] = jnp.dot(
                pick, part, preferred_element_type=F32
            ).astype(BF16)

    def norm_rows(load, shift, scale):
        def body(i, carry):
            rows = pl.ds(pl.multiple_of(i * 32, 32), 32)
            v = load(rows)
            mean = jnp.sum(v, axis=-1, keepdims=True) * (1.0 / D)
            v = v - mean
            var = jnp.sum(v * v, axis=-1, keepdims=True) * (1.0 / D)
            normed = v * lax.rsqrt(var + 1e-6)
            h[rows, :] = (normed * (1.0 + scale[...]) + shift[...]).astype(BF16)
            return carry
        lax.fori_loop(0, 8, body, 0)

    def times(lhs_ref, c0, width):
        return jnp.dot(
            lhs_ref[:, :MAIN], wall[:, :, :, pl.ds(c0, width)].reshape(MAIN, width), preferred_element_type=F32
        ) + jnp.dot(lhs_ref[:, MAIN:], wrem[:, pl.ds(c0, width)], preferred_element_type=F32)

    def times_t(load, dst, j, c0, width):
        def body(zz, carry):
            w = wall[zz, :, :, pl.ds(c0, width)].reshape(256, width)
            dst[j, :, pl.ds(pl.multiple_of(zz * 256, 256), 256)] = lax.dot_general(
                load(), w, NT, preferred_element_type=F32
            ).astype(BF16)
            return carry
        lax.fori_loop(0, 4, body, 0)
        dst[j, :, MAIN:] = lax.dot_general(
            load(), wrem[:, pl.ds(c0, width)], NT, preferred_element_type=F32
        ).astype(BF16)

    def col_copy(own, got, j, base):
        return rdma(own.at[j], got.at[j], col_send.at[base + j], col_recv.at[base + j], col_dev)

    def pass_copy(j):
        return rdma(y.at[j], x.at[j], pass_send.at[j], pass_recv.at[j], sec_dev)

    arrived(1)

    @pl.when(sec == 0)
    def _():
        x_theirs = x.at[:, pl.ds((1 - col) * 128, 128)]
        rdma(lat_ref, x_theirs, pass_send.at[4], pass_recv.at[4], col_dev).wait_recv()

    def attend_step(j, carry):
        @pl.when(sec == 1)
        def _():
            pass_copy(j).wait_recv()

        norm_rows(lambda rows: x[j, rows, :].astype(F32), mod_ref.at[0:1], mod_ref.at[1:2])
        qs[...] = times(h, 0, HEADW).astype(BF16)
        kbuf[j] = times(h, HEADW, HEADW).astype(BF16)
        vbuf[j] = times(h, 2 * HEADW, HEADW).astype(BF16)

        def heads(p, c):
            window = pl.ds(pl.multiple_of(p * 128, 128), 256)
            q_win = qs[:, window]
            k_win = kbuf[:, :, window].reshape(1024, 256)
            v_win = vbuf[:, :, window].reshape(1024, 256)
            lane = lax.broadcasted_iota(jnp.int32, (256, 256), 1) - p * 16
            mixed = att[:, window].astype(F32)
            for e in (0, 1):
                mine = (lane >= e * HD) & (lane < (e + 1) * HD)
                scores = lax.dot_general(
                    jnp.where(mine, q_win.astype(F32), 0.0).astype(BF16), k_win, NT, preferred_element_type=F32
                ) * (1.0 / math.sqrt(HD))
                scores = jnp.where(valid_ref[...] > 0, scores, -1e30)
                weights = jnp.exp(scores - jnp.max(scores, axis=-1, keepdims=True))
                totals = jnp.sum(weights, axis=-1, keepdims=True)
                got = jnp.dot(weights.astype(BF16), v_win, preferred_element_type=F32)
                mixed = jnp.where(mine, got / totals, mixed)
            att[:, window] = mixed.astype(BF16)
            return c
        lax.fori_loop(0, 4, heads, 0)
        times_t(lambda: att[...], pa_own, j, COL_OUT, HEADW)
        col_copy(pa_own, pa_got, j, 0).start()
        return carry
    lax.fori_loop(0, 4, attend_step, 0)

    arrived(2)

    def up_step(j, carry):
        col_copy(pa_own, pa_got, j, 0).wait_recv()

        def load(rows):
            v = x[j, rows, :].astype(F32) + mod_ref[2:3] * (
                pa_own[j, rows, :].astype(F32) + pa_got[j, rows, :].astype(F32)
            )
            x1[j, rows, :] = v
            return v
        norm_rows(load, mod_ref.at[3:4], mod_ref.at[4:5])

        def body(n, c):
            u = times(h, pl.multiple_of(COL_UP + n * 256, 256), 256)
            g = 0.5 * u * (1.0 + jnp.tanh(math.sqrt(2.0 / math.pi) * (u + 0.044715 * (u * u * u))))
            hid[j, :, pl.ds(pl.multiple_of(n * 256, 256), 256)] = g.astype(BF16)
            return c
        lax.fori_loop(0, 9, body, 0)
        return carry
    lax.fori_loop(0, 4, up_step, 0)

    arrived(3)

    def finish(j):
        col_copy(pm_own, pm_got, j, 4).wait_recv()

        def body(i, c):
            rows = pl.ds(pl.multiple_of(i * 32, 32), 32)
            y[j, rows, :] = (
                x1[j, rows, :]
                + mod_ref[5:6] * (pm_own[j, rows, :].astype(F32) + pm_got[j, rows, :].astype(F32))
            ).astype(BF16)
            return c
        lax.fori_loop(0, 8, body, 0)

        @pl.when(sec == 0)
        def _():
            pass_copy(j).start()
        out_ref[j] = y[j, pl.ds(col * 128, 128), :]

    def down_step(j, carry):
        times_t(lambda: hid[j], pm_own, j, COL_DOWN, 2304)
        col_copy(pm_own, pm_got, j, 4).start()

        @pl.when(j > 0)
        def _():
            finish(j - 1)
        return carry
    lax.fori_loop(0, 4, down_step, 0)
    finish(3)

    for k in pieces:
        xh_copy(k).wait_send()
        for phase in (0, 1):
            for half in (0, 1):
                for d in (1, 2, 3):
                    ring_copy(k, half, phase, d, False).wait_send()

    def drain(j, c):
        col_copy(pa_own, pa_got, j, 0).wait_send()
        col_copy(pm_own, pm_got, j, 4).wait_send()

        @pl.when(sec == 0)
        def _():
            pass_copy(j).wait_send()
        return c
    lax.fori_loop(0, 4, drain, 0)

    @pl.when(sec == 0)
    def _():
        rdma(lat_ref, x_mine, pass_send.at[4], pass_recv.at[4], col_dev).wait_send()


def run_relay(valid, mod, lat, stale_k, stale_v, main, rem):
    vmem = pl.BlockSpec(memory_space=pltpu.VMEM)
    tokens = (4, 256, D)
    return pl.pallas_call(
        relay,
        out_shape=jax.ShapeDtypeStruct((4, 128, D), BF16),
        in_specs=[vmem] * 7,
        out_specs=vmem,
        scratch_shapes=[
            pltpu.VMEM((4, 4, 64, COLS), BF16),
            pltpu.VMEM((4, 4, 32, QUARTER), BF16),
            pltpu.VMEM((128, COLS), BF16),
            pltpu.VMEM(tokens, BF16),
            pltpu.VMEM(tokens, F32),
            pltpu.VMEM((256, HEADW), BF16),
            pltpu.VMEM((4, 256, HEADW), BF16),
            pltpu.VMEM((4, 256, HEADW), BF16),
            pltpu.VMEM((256, HEADW), BF16),
            pltpu.VMEM((4, 256, 2304), BF16),
            pltpu.VMEM((256, D), BF16),
            pltpu.VMEM(tokens, BF16),
            pltpu.VMEM(tokens, BF16),
            pltpu.VMEM(tokens, BF16),
            pltpu.VMEM(tokens, BF16),
            pltpu.VMEM(tokens, BF16),
            pltpu.SemaphoreType.DMA((2,)),
            pltpu.SemaphoreType.DMA((4,)),
            pltpu.SemaphoreType.DMA((4,)),
            pltpu.SemaphoreType.DMA((48,)),
            pltpu.SemaphoreType.DMA((48,)),
            pltpu.SemaphoreType.DMA((8,)),
            pltpu.SemaphoreType.DMA((8,)),
            pltpu.SemaphoreType.DMA((5,)),
            pltpu.SemaphoreType.DMA((5,)),
        ],
        compiler_params=pltpu.CompilerParams(
            collective_id=0, has_side_effects=True, vmem_limit_bytes=67043328
        ),
    )(valid, mod, lat, stale_k, stale_v, main, rem)


def local(
    latents,
    timesteps,
    lengths,
    patch_order,
    ada_weight,
    qkv_weight,
    out_weight,
    up_weight,
    down_weight,
    stale_keys,
    stale_values,
):
    row = lax.axis_index("row")
    rows = D // 32

    steps = lax.all_gather(timesteps, "row", axis=0, tiled=True)
    cond = jax.nn.silu(sinusoid(steps)).astype(BF16)
    cond = lax.dynamic_slice_in_dim(cond, row * rows, rows, axis=1)
    partial = jnp.einsum("rd,dkc->rkc", cond, ada_weight[0], preferred_element_type=F32)
    mod = lax.psum_scatter(partial, "row", scatter_dimension=0, tiled=True)
    mod = lax.all_gather(mod, "col", axis=2, tiled=True)
    mod = mod.reshape(6, 32, 36)
    mod = jnp.concatenate([mod[:, :, :32].reshape(6, MAIN), mod[:, :, 32:].reshape(6, 128)], axis=1)

    place = jnp.arange(D, dtype=jnp.int32)
    rest = place - MAIN
    source = jnp.where(place < MAIN, (place // 32) * 36 + place % 32, (rest // 4) * 36 + 32 + rest % 4)
    order = (place[:, None] == source[None, :]).astype(BF16)
    lat = jnp.take(latents[0], patch_order, axis=0)
    lat = jnp.einsum("ptd,de->pte", lat, order, preferred_element_type=F32).astype(BF16)

    pad = lambda a, n: jnp.pad(a, ((0, 0), (0, n - a.shape[1])))
    shard = jnp.concatenate(
        [pad(qkv_weight[0, :, i], HEADW) for i in range(3)]
        + [pad(out_weight[0].T, HEADW), up_weight[0], down_weight[0].T],
        axis=1,
    )
    main = shard[:32]
    rem = shard[32:].reshape(4, 4, QUARTER).transpose(1, 0, 2).reshape(16, QUARTER)

    wide = lambda a: jnp.pad(jnp.take(a, patch_order, axis=0), ((0, 0), (0, 0), (0, HEADW - a.shape[2])))
    position = patch_order[:, None] * 256 + jnp.arange(256, dtype=jnp.int32)[None, :]
    valid = (position < lengths[0]).astype(jnp.int32).reshape(1, 1024)

    out = run_relay(valid, mod, lat, wide(stale_keys[0, 0]), wide(stale_values[0, 0]), main, rem)
    out = jnp.einsum("pte,de->ptd", out, order, preferred_element_type=F32).astype(BF16)
    where = jnp.argmax(patch_order[None, :] == jnp.arange(4, dtype=jnp.int32)[:, None], axis=1)
    return jnp.take(out, where, axis=0)[None, None]


def solution(mesh):
    return jax.shard_map(
        local,
        mesh=mesh,
        in_specs=(
            P("row", None, "col", None),
            P("row"),
            P("row"),
            P(),
            P("section", "row", None, "col"),
            P("section", "row", None, "col"),
            P("section", "col", "row"),
            P("section", "row", "col"),
            P("section", "col", "row"),
            P("section", "row", None, None, "col"),
            P("section", "row", None, None, "col"),
        ),
        out_specs=P("section", "row", None, "col", None),
        check_vma=False,
    )
```

time: 1010 us -> 644 us (0.64)
  waiting for transfers between devices: 619 us -> 308 us
  Pallas kernels: 0 us -> 264 us
  local copies, waits for them, and re-layouts: 121 us -> 16.4 us
  matrix products: 96.2 us -> 8.19 us
  blocking collectives: 89 us -> 25.4 us
  other arithmetic: 51 us -> 5.73 us
  between operations: 25.1 us -> 15 us
    all_gather x5 -> x0, waiting for transfers between devices: 434 us -> none  [the longest x1 115 us: local(): lax.all_gather(ada_local, 'row', axis=0, tiled=True)]
    unnamed x15 -> x2, waiting for transfers between devices: 0.24 us -> 308 us
    pallas_call x0 -> x1, Pallas kernels: none -> 264 us  [run_relay(): pl.pallas_call(relay, out_shape=jax.ShapeDtypeStruct((4, 128, D), BF16),...]
    reduce_scatter x10 -> x0, waiting for transfers between devices: 184 us -> none  [the longest x5 93.3 us: local(): lax.psum_scatter(mlp_partial.astype(jnp.bfloat16), 'col', scatter_dimensi...]
    dot_general x26 -> x3, matrix products: 96.2 us -> 8.19 us  [the longest x1 3.16 us: local(): jnp.einsum('pte,de->ptd', out, order, preferred_element_type=F32)]
    all_gather x11 -> x1, blocking collectives: 89 us -> 6.77 us  [local(): mod = lax.all_gather(mod, 'col', axis=2, tiled=True)]
    all_gather x4 -> x1, local copies, waits for them, and re-layouts: 42 us -> 0.48 us  [local(): mod = lax.all_gather(mod, 'col', axis=2, tiled=True)]
    another operation x10 -> x0, local copies, waits for them, and re-layouts: 33 us -> none
  transfers between devices with their start and end apart: 19 -> 1, of which waited for: 19 -> 1; matrix products, arithmetic and copies ran while one was open for 10% -> 3% of each run, Pallas kernels for 0% -> 0%
where the time goes in v1:
time: 644 us; the launch traced here: 643 us
  waiting for transfers between devices  308 us (48%)
  Pallas kernels  264 us (41%)
  blocking collectives  25.4 us (4%)
  local copies, waits for them, and re-layouts  16.4 us (3%)
  between operations  15 us (2%)
  matrix products  8.19 us (1%)
    unnamed x2, waiting for transfers between devices  308 us
    pallas_call x1, Pallas kernels, run_relay(): pl.pallas_call(relay, out_shape=jax.ShapeDtypeStruct((4, 128, D), BF16),...  264 us
    unnamed x1, blocking collectives  18.7 us
  transfers between devices with their start and end apart: 1, of which 1 were waited for; matrix products, arithmetic and copies ran while one was open for 3% of the time, Pallas kernels for 0%

profile of v1, /device:TPU:1, one launch (start us, length us, event | category | flops | bytes accessed | tf_op | source)
XLA Modules:
  0.0 643.2 jit_solution(8609734445720200219)
XLA Ops:
  6.5 0.0 all-reduce.10.cloned.1.call-start
  7.3 1.3 fusion.45
  8.6 0.8 dynamic-update-slice
  9.3 18.7 %all-reduce.6 = s32[32]{0:T(128)S(1)} all-reduce(s32[32]{0:T(128)S(1)} %dynamic-update-slice), channel_id=1, replica_groups=mesh['section'=2,'row'=32,'col'=2] {'row'}, use_global_device_ids=true, to_apply=%add.6 | all-reduce | flops 32 | bytes 256
  28.0 0.4 multiply_cosine_fusion
  28.4 0.0 copy-start.3
  28.4 2.1 fusion.16
  30.5 0.0 all-reduce.10.cloned.1.call-update
  30.5 0.0 copy-done.8
  30.5 0.6 iota_reduce_fusion
  31.1 0.5 compare_and_fusion
  31.7 0.0 copy-done.4
  31.7 0.0 copy-start.6
  31.7 0.0 copy-start
  31.8 0.0 copy-done.5
  31.8 0.0 copy-done.2
  31.9 0.8 slice.38.main_ref
  32.7 0.4 copy-done
  33.1 0.6 gather_fusion.1
  33.8 0.7 copy.29
  34.5 1.9 gather_fusion.2
  36.4 1.5 copy.30
  37.8 1.7 broadcast_select_fusion
  39.5 1.2 pad.20.stale_k
  40.7 1.2 pad.21.stale_v
  41.9 0.5 copy-done.1
  42.5 0.7 gather_fusion
  43.2 0.6 reshape.127.rem_ref
  44.5 0.1 convert_bitcast_fusion
  44.6 0.6 copy.34
  45.2 0.6 pad_clamp_fusion
  45.8 0.0 copy-done.6
  45.8 2.9 fusion.5.lat_ref
  48.7 308.0 %all-reduce.10.cloned.1.call-done = f32[32,6,576]{2,0,1:T(8,128)} async-done(((f32[32,6,576]{2,0,1:T(8,128)}), f32[32,6,576]{2,0,1:T(8,128)}) %all-reduce.10.cloned.1.call-update) | async-done | bytes 442384
  356.7 1.5 constant_dynamic-slice_fusion
  358.2 0.2 copy.27
  358.4 6.8 %all_gather.7 = f32[1,6,1152]{1,0,2:T(1,128)S(1)} all-gather(f32[1,6,576]{1,0,2:T(1,128)S(1)} %copy.27), channel_id=1, replica_groups=mesh['section'=2,'row'=32,'col'=2] {'col'}, dimensions={2}, use_global_device_ids=true | all-gather | bytes 41472 | tf_op jit(solution)/shard_map/all_gather | solution.py:393
  365.1 0.5 copy.28
  365.6 0.1 reshape.123
  365.8 0.1 slice.37
  365.9 0.1 reshape.125
  366.0 0.1 reshape.124
  366.1 0.6 pad_maximum_fusion.mod_ref
  366.7 264.4 %shard_map.109 = bf16[4,128,1152]{2,1,0:T(8,128)(2,1)} custom-call(s32[1,1024]{1,0:T(1,128)} %bitcast.53, f32[6,1152]{1,0:T(8,128)} %pad_maximum_fusion.mod_ref, bf16[4,128,1152]{2,1,0:T(8,128)(2,1)} %fusion.5.lat_ref, bf16[4,256,640]{2,1,0:T(8,128)(2,1)} %pad.20.stale_k, bf16[4,256,640]{2,1,0:T(8,128)(2,1)} %pad.21.stale_v, ...), custom_call_target="tpu_custom_call" | custom-call | tf_op jit(solution)/shard_map/pallas_call | solution.py:334
  631.1 3.2 fusion.8
  634.3 0.0 copy-start.7
  634.3 0.9 gather_fusion.3
  635.2 1.2 select_bitcast_fusion
  (21 shorter events, 0.2 us)
Async XLA Ops:
  6.5 24.0 %copy-start.8 = (s32[4]{0:T(128)S(1)}, s32[4]{0:T(128)}, u32[]{:S(2)}) copy-start(s32[4]{0:T(128)} %param.18) | copy-start | bytes 52
  6.5 25.1 %copy-start.4 = (bf16[1,36,3,576]{3,1,2,0:T(8,128)(2,1)S(1)}, bf16[1,36,3,576]{3,1,2,0:T(8,128)(2,1)}, u32[]{:S(2)}) copy-start(bf16[1,36,3,576]{3,1,2,0:T(8,128)(2,1)} %param.20) | copy-start | bytes 373252
  6.5 25.3 %copy-start.5 = (bf16[1,576,36]{1,2,0:T(8,128)(2,1)S(1)}, bf16[1,576,36]{1,2,0:T(8,128)(2,1)}, u32[]{:S(2)}) copy-start(bf16[1,576,36]{1,2,0:T(8,128)(2,1)} %param.21) | copy-start | bytes 124420
  6.5 350.2 %all-reduce.10.cloned.1.call-start = ((), (), s32[]{:S(2)}) async-start(), calls=%async_computation | async-start | bytes 983040
  28.0 3.8 copy-start.2
  28.4 3.5 copy-start.3
  31.7 14.1 %copy-start.6 = (s32[1152]{0:T(1024)}, s32[1152]{0:T(1024)S(1)}, u32[]{:S(2)}) copy-start(s32[1152]{0:T(1024)S(1)} %fusion.31) | copy-start | bytes 13828
  31.7 1.4 copy-start
  40.7 1.7 copy-start.1
  634.3 0.9 copy-start.7
Sparse Core Ops, SparseCore 0:
  30.6 326.0 all-reduce.9

commit v2 on v1

--- a/solution.py
+++ b/solution.py
@@ -18,6 +18,7 @@
 COL_DOWN = COL_UP + 2304
 COLS = COL_DOWN + 2304
 QUARTER = COLS // 4
+MODW = 6 * HEADW
 CHUNKS = ((0, COL_UP), (COL_UP, COL_DOWN), (COL_DOWN, COLS))
 MAIN = 1024
 MESH = pl.DeviceIdType.MESH
@@ -38,9 +39,10 @@
 
 
 def relay(
-    valid_ref, mod_ref, lat_ref, stale_k, stale_v, main_ref, rem_ref, out_ref,
+    valid_ref, cond_ref, ada_ref, lat_ref, stale_k, stale_v, main_ref, rem_ref, out_ref,
+    cbuf, cmat, part, got_z, sum_z, got_y, sum_y, got_x, mod_own, mod_got, mod_ref,
     wall, stag, wrem, x, x1, qs, kbuf, vbuf, att, hid, h, pa_own, pa_got, pm_own, pm_got, y,
-    local_sem, xh_send, xh_recv, send_sem, recv_sem, col_send, col_recv, pass_send, pass_recv,
+    cond_send, cond_recv, sum_send, sum_recv, local_sem, xh_send, xh_recv, send_sem, recv_sem, col_send, col_recv, pass_send, pass_recv,
 ):
     sec = lax.axis_index("section")
     row = lax.axis_index("row")
@@ -129,6 +131,10 @@
 
     own_main = pltpu.make_async_copy(main_ref, wall.at[z, yy, pl.ds(xh * 32, 32)], local_sem.at[0])
     own_rem = pltpu.make_async_copy(rem_ref, stag.at[z, yy, pl.ds(xh * 16, 16)], local_sem.at[1])
+    own_cond = pltpu.make_async_copy(cond_ref, cbuf.at[z, yy, pl.ds(xh * 32, 32)], local_sem.at[2])
+    own_cond.start()
+    cond_xh = rdma(cond_ref, cbuf.at[z, yy, pl.ds(xh * 32, 32)], cond_send.at[0], cond_recv.at[0], xh_dev)
+    cond_xh.start()
     own_main.start()
     own_rem.start()
     for k in pieces:
@@ -144,6 +150,55 @@
     kbuf[...] = stale_k[...]
     vbuf[...] = stale_v[...]
     att[...] = jnp.zeros_like(att)
+
+    own_cond.wait()
+    rdma(
+        cond_ref, cbuf.at[z, yy, pl.ds((1 - xh) * 32, 32)], cond_send.at[0], cond_recv.at[0], xh_dev
+    ).wait_recv()
+
+    def cond_y(d, arrival):
+        ref = cbuf.at[z, y_peer[4 - d] if arrival else yy]
+        return rdma(ref, ref, cond_send.at[d], cond_recv.at[d], at(y_=y_peer[d]))
+
+    def cond_z(d, arrival):
+        ref = cbuf.at[z_peer[4 - d] if arrival else z]
+        return rdma(ref, ref, cond_send.at[3 + d], cond_recv.at[3 + d], at(zz=z_peer[d]))
+
+    def part_z(d):
+        return rdma(part.at[z_peer[d]], got_z.at[d - 1], sum_send.at[d - 1], sum_recv.at[d - 1], at(zz=z_peer[d]))
+
+    def part_y(d):
+        return rdma(sum_z.at[y_peer[d]], got_y.at[d - 1], sum_send.at[d + 2], sum_recv.at[d + 2], at(y_=y_peer[d]))
+
+    for d in (1, 3, 2):
+        cond_y(d, False).start()
+    for d in (1, 3, 2):
+        cond_y(d, True).wait_recv()
+    for d in (1, 3, 2):
+        cond_z(d, False).start()
+    for d in (1, 3, 2):
+        cond_z(d, True).wait_recv()
+    for i in range(32):
+        cmat[i:i + 1, :] = cbuf[i // 8, (i // 2) % 4, pl.ds((i % 2) * 32 + row, 1), :]
+    products = jnp.dot(cmat[...].astype(BF16), ada_ref[...], preferred_element_type=F32)
+    for i in range(32):
+        part[i // 8, (i // 2) % 4, i % 2] = products[i:i + 1, :]
+    for d in (1, 3, 2):
+        part_z(d).start()
+    for d in (1, 3, 2):
+        part_z(d).wait_recv()
+    sum_z[...] = part[z] + got_z[0] + got_z[1] + got_z[2]
+    for d in (1, 3, 2):
+        part_y(d).start()
+    for d in (1, 3, 2):
+        part_y(d).wait_recv()
+    sum_y[...] = sum_z[yy] + got_y[0] + got_y[1] + got_y[2]
+    part_x = rdma(sum_y.at[1 - xh], got_x, sum_send.at[6], sum_recv.at[6], xh_dev)
+    part_x.start()
+    part_x.wait_recv()
+    mod_own[...] = sum_y[xh] + got_x[...]
+    mod_copy = rdma(mod_own, mod_got, sum_send.at[7], sum_recv.at[7], col_dev)
+    mod_copy.start()
 
     own_main.wait()
     own_rem.wait()
@@ -164,6 +219,13 @@
             for d in (1, 2, 3):
                 ring_copy(k, half, 1, d, True).wait_recv()
 
+    mod_copy.wait_recv()
+    for k in range(6):
+        base = k * HEADW
+        mod_ref[k:k + 1, pl.ds(col * 512, 512)] = mod_own[:, base:base + 512]
+        mod_ref[k:k + 1, pl.ds((1 - col) * 512, 512)] = mod_got[:, base:base + 512]
+        mod_ref[k:k + 1, MAIN:] = mod_own[:, base + 512:base + HEADW] + mod_got[:, base + 512:base + HEADW]
+
     arrived(0)
     rows_i = lax.broadcasted_iota(jnp.int32, (128, 512), 0)
     cols_i = lax.broadcasted_iota(jnp.int32, (128, 512), 1)
@@ -172,9 +234,9 @@
             ((cols_i >> 4) == (rows_i >> 2)) & ((cols_i & 15) == 4 * q + (rows_i & 3)), 1.0, 0.0
         ).astype(BF16)
         for n in range(QUARTER // 256):
-            part = stag[:, :, :, n * 256:(n + 1) * 256].reshape(512, 256)
+            rest = stag[:, :, :, n * 256:(n + 1) * 256].reshape(512, 256)
             wrem[:, q * QUARTER + n * 256:q * QUARTER + (n + 1) * 256] = jnp.dot(
-                pick, part, preferred_element_type=F32
+                pick, rest, preferred_element_type=F32
             ).astype(BF16)
 
     def norm_rows(load, shift, scale):
@@ -306,6 +368,14 @@
     lax.fori_loop(0, 4, down_step, 0)
     finish(3)
 
+    cond_xh.wait_send()
+    for d in (1, 2, 3):
+        cond_y(d, False).wait_send()
+        cond_z(d, False).wait_send()
+        part_z(d).wait_send()
+        part_y(d).wait_send()
+    part_x.wait_send()
+    mod_copy.wait_send()
     for k in pieces:
         xh_copy(k).wait_send()
         for phase in (0, 1):
@@ -328,15 +398,26 @@
         rdma(lat_ref, x_mine, pass_send.at[4], pass_recv.at[4], col_dev).wait_send()
 
 
-def run_relay(valid, mod, lat, stale_k, stale_v, main, rem):
+def run_relay(valid, cond, ada, lat, stale_k, stale_v, main, rem):
     vmem = pl.BlockSpec(memory_space=pltpu.VMEM)
     tokens = (4, 256, D)
     return pl.pallas_call(
         relay,
         out_shape=jax.ShapeDtypeStruct((4, 128, D), BF16),
-        in_specs=[vmem] * 7,
+        in_specs=[vmem] * 8,
         out_specs=vmem,
         scratch_shapes=[
+            pltpu.VMEM((4, 4, 64, 128), F32),
+            pltpu.VMEM((32, 128), F32),
+            pltpu.VMEM((4, 4, 2, 1, MODW), F32),
+            pltpu.VMEM((3, 4, 2, 1, MODW), F32),
+            pltpu.VMEM((4, 2, 1, MODW), F32),
+            pltpu.VMEM((3, 2, 1, MODW), F32),
+            pltpu.VMEM((2, 1, MODW), F32),
+            pltpu.VMEM((1, MODW), F32),
+            pltpu.VMEM((1, MODW), F32),
+            pltpu.VMEM((1, MODW), F32),
+            pltpu.VMEM((8, D), F32),
             pltpu.VMEM((4, 4, 64, COLS), BF16),
             pltpu.VMEM((4, 4, 32, QUARTER), BF16),
             pltpu.VMEM((128, COLS), BF16),
@@ -353,7 +434,11 @@
             pltpu.VMEM(tokens, BF16),
             pltpu.VMEM(tokens, BF16),
             pltpu.VMEM(tokens, BF16),
-            pltpu.SemaphoreType.DMA((2,)),
+            pltpu.SemaphoreType.DMA((7,)),
+            pltpu.SemaphoreType.DMA((7,)),
+            pltpu.SemaphoreType.DMA((8,)),
+            pltpu.SemaphoreType.DMA((8,)),
+            pltpu.SemaphoreType.DMA((3,)),
             pltpu.SemaphoreType.DMA((4,)),
             pltpu.SemaphoreType.DMA((4,)),
             pltpu.SemaphoreType.DMA((48,)),
@@ -366,7 +451,7 @@
         compiler_params=pltpu.CompilerParams(
             collective_id=0, has_side_effects=True, vmem_limit_bytes=67043328
         ),
-    )(valid, mod, lat, stale_k, stale_v, main, rem)
+    )(valid, cond, ada, lat, stale_k, stale_v, main, rem)
 
 
 def local(
@@ -382,17 +467,16 @@
     stale_keys,
     stale_values,
 ):
-    row = lax.axis_index("row")
-    rows = D // 32
-
-    steps = lax.all_gather(timesteps, "row", axis=0, tiled=True)
-    cond = jax.nn.silu(sinusoid(steps)).astype(BF16)
-    cond = lax.dynamic_slice_in_dim(cond, row * rows, rows, axis=1)
-    partial = jnp.einsum("rd,dkc->rkc", cond, ada_weight[0], preferred_element_type=F32)
-    mod = lax.psum_scatter(partial, "row", scatter_dimension=0, tiled=True)
-    mod = lax.all_gather(mod, "col", axis=2, tiled=True)
-    mod = mod.reshape(6, 32, 36)
-    mod = jnp.concatenate([mod[:, :, :32].reshape(6, MAIN), mod[:, :, 32:].reshape(6, 128)], axis=1)
+    cond = jax.nn.silu(sinusoid(timesteps)).astype(BF16).astype(F32)
+    cond = jnp.pad(cond.reshape(32, 36), ((0, 0), (0, 92)))
+    from_col = jnp.arange(576, dtype=jnp.int32)
+    group, inner = from_col // 36, from_col % 36
+    to_col = jnp.where(
+        inner < 32, group * 32 + inner, 512 + 64 * lax.axis_index("col") + group * 4 + inner - 32
+    )
+    spread = (to_col[:, None] == jnp.arange(HEADW, dtype=jnp.int32)[None, :]).astype(BF16)
+    ada = jnp.einsum("dkc,ce->dke", ada_weight[0], spread, preferred_element_type=F32).astype(BF16)
+    ada = jnp.pad(ada.reshape(36, MODW), ((0, 92), (0, 0)))
 
     place = jnp.arange(D, dtype=jnp.int32)
     rest = place - MAIN
@@ -414,7 +498,7 @@
     position = patch_order[:, None] * 256 + jnp.arange(256, dtype=jnp.int32)[None, :]
     valid = (position < lengths[0]).astype(jnp.int32).reshape(1, 1024)
 
-    out = run_relay(valid, mod, lat, wide(stale_keys[0, 0]), wide(stale_values[0, 0]), main, rem)
+    out = run_relay(valid, cond, ada, lat, wide(stale_keys[0, 0]), wide(stale_values[0, 0]), main, rem)
     out = jnp.einsum("pte,de->ptd", out, order, preferred_element_type=F32).astype(BF16)
     where = jnp.argmax(patch_order[None, :] == jnp.arange(4, dtype=jnp.int32)[:, None], axis=1)
     return jnp.take(out, where, axis=0)[None, None]

time: 644 us -> 300 us (0.47)
  waiting for transfers between devices: 308 us -> 0 us
  blocking collectives: 25.4 us -> 0 us
  between operations: 15 us -> 1.55 us
    unnamed x2 -> x0, waiting for transfers between devices: 308 us -> none
    unnamed x1 -> x0, blocking collectives: 18.7 us -> none
    all_gather x1 -> x0, blocking collectives: 6.77 us -> none  [local(): mod = lax.all_gather(mod, 'col', axis=2, tiled=True)]
  transfers between devices with their start and end apart: 1 -> 0, of which waited for: 1 -> 0; matrix products, arithmetic and copies ran while one was open for 3% -> 0% of each run, Pallas kernels for 0% -> 0%
where the time goes in v2:
time: 300 us
  Pallas kernels  270 us (90%)
  local copies, waits for them, and re-layouts  14.7 us (5%)
  matrix products  6.7 us (2%)
  other arithmetic  6.32 us (2%)
    pallas_call x1, Pallas kernels, run_relay(): pl.pallas_call(relay, out_shape=jax.ShapeDtypeStruct((4, 128, D), BF16),...  270 us

profile of v2, /device:TPU:1, one launch (start us, length us, event | category | flops | bytes accessed | tf_op | source)
XLA Modules:
  0.0 299.6 jit_solution(851994176927061278)
XLA Ops:
  0.0 1.3 iota_reduce_fusion
  1.3 0.0 copy-start.8
  1.3 0.5 copy-done.8
  1.8 0.7 compare_select_fusion.1
  2.5 0.6 pad_clamp_fusion
  3.1 1.9 gather_fusion.1
  5.0 0.7 copy.19
  5.7 1.9 gather_fusion.2
  7.6 0.0 copy-start.7
  7.6 1.5 copy.20
  9.0 0.0 copy-done.7
  9.1 1.7 broadcast_select_fusion
  10.7 1.2 pad.33.stale_k
  11.9 0.0 copy-start.3
  11.9 0.0 copy-start.4
  11.9 0.0 copy-start.1
  11.9 1.2 pad.34.stale_v
  13.1 0.0 copy-done.3
  13.1 0.0 copy-start.2
  13.2 0.0 copy-start
  13.2 0.0 copy-done.4
  13.3 0.0 copy-done.1
  13.3 0.8 copy-done.2
  14.1 0.8 slice.28.main_ref
  14.9 0.6 reshape.178.rem_ref
  15.6 0.0 copy-done
  15.6 0.7 gather_fusion
  16.3 0.0 copy-start.5
  16.3 0.0 copy-start.6
  16.3 3.0 fusion.5.lat_ref
  19.3 0.0 copy-done.5
  19.9 0.1 fusion.54
  20.1 0.1 maximum_reduce_fusion
  20.1 0.1 concatenate.13
  20.3 0.6 pad_convert_fusion.cond_ref
  21.5 0.1 convert_bitcast_fusion
  21.6 0.6 copy.22
  22.2 0.0 copy-done.6
  22.2 0.6 fusion.19
  22.9 0.1 pad.45
  23.0 1.0 pad.32.ada_ref
  24.0 270.3 %shard_map.109 = bf16[4,128,1152]{2,1,0:T(8,128)(2,1)} custom-call(s32[1,1024]{1,0:T(1,128)} %bitcast.61, f32[32,128]{1,0:T(8,128)} %pad_convert_fusion.cond_ref, bf16[128,3840]{1,0:T(8,128)(2,1)} %pad.32.ada_ref, bf16[4,128,1152]{2,1,0:T(8,128)(2,1)} %fusion.5.lat_ref, bf16[4,256,640]{2,1,0:T(8,128)(2,1)} %pad.33.stale_k, ...), custom_call_target="tpu_custom_call" | custom-call | tf_op jit(solution)/shard_map/pallas_call | solution.py:404
  294.4 3.2 %fusion.8 = bf16[4,128,1152]{2,1,0:T(8,128)(2,1)S(1)} fusion(bf16[4,128,1152]{2,1,0:T(8,128)(2,1)} %shard_map.109, s32[1152]{0:T(1024)} %copy-done.5), kind=kOutput, calls=%fused_computation.9 | convolution fusion | flops 1360871424 | bytes 2363904 | tf_op jit(solution)/shard_map/pte,de->ptd/dot_general | solution.py:502
  297.5 0.0 copy-start.9
  297.5 0.9 gather_fusion.3
  298.4 0.0 copy-done.9
  298.4 1.2 select_bitcast_fusion
  (16 shorter events, 0.3 us)
Async XLA Ops:
  1.3 0.5 copy-start.8
  7.6 1.5 copy-start.7
  11.9 1.2 copy-start.3
  11.9 1.3 copy-start.4
  11.9 1.3 copy-start.1
  13.1 0.9 copy-start.2
  13.2 2.4 copy-start
  16.3 3.0 copy-start.5
  16.3 5.9 %copy-start.6 = (bf16[1,36,6,576]{3,1,2,0:T(8,128)(2,1)S(1)}, bf16[1,36,6,576]{3,1,2,0:T(8,128)(2,1)}, u32[]{:S(2)}) copy-start(bf16[1,36,6,576]{3,1,2,0:T(8,128)(2,1)} %param.19) | copy-start | bytes 746500
  297.5 0.9 copy-start.9

commit v3 on v2

--- a/solution.py
+++ b/solution.py
@@ -39,10 +39,11 @@
 
 
 def relay(
-    valid_ref, cond_ref, ada_ref, lat_ref, stale_k, stale_v, main_ref, rem_ref, out_ref,
+    place_ref, slot_ref, length_ref, cond_ref, ada_ref, lat_ref, stale_k, stale_v, main_ref, rem_ref, out_ref,
+    order, valid_ref, latp, yout,
     cbuf, cmat, part, got_z, sum_z, got_y, sum_y, got_x, mod_own, mod_got, mod_ref,
     wall, stag, wrem, x, x1, qs, kbuf, vbuf, att, hid, h, pa_own, pa_got, pm_own, pm_got, y,
-    cond_send, cond_recv, sum_send, sum_recv, local_sem, xh_send, xh_recv, send_sem, recv_sem, col_send, col_recv, pass_send, pass_recv,
+    cond_send, cond_recv, sum_send, sum_recv, go_sem, local_sem, xh_send, xh_recv, send_sem, recv_sem, col_send, col_recv, pass_send, pass_recv,
 ):
     sec = lax.axis_index("section")
     row = lax.axis_index("row")
@@ -104,30 +105,45 @@
             xh_send.at[k], xh_recv.at[k], xh_dev,
         )
 
-    def block(k, half, phase, zz, y_):
+    def ring_copy(k, half, phase, link, arrival):
+        i = ((phase * 2 + half) * 4 + k) * 4 + link
+        along_y = (half == 0) == (phase == 0)
+        ahead = link % 2 == 0
+        peers = y_peer if along_y else z_peer
+        dev = at(y_=peers[1 if ahead else 3]) if along_y else at(zz=peers[1 if ahead else 3])
+        if arrival:
+            member = peers[(3 if ahead else 1) if link < 2 else 2]
+        else:
+            member = peers[0 if link < 2 else (3 if ahead else 1)]
+        c0, width = span(k, half)
+        if link >= 2:
+            first = (width // 256) * 128 if (width // 128) % 2 == 0 else (width // 256 + 1) * 128
+            c0, width = (c0, first) if ahead else (c0 + first, width - first)
         ref = buf(k)[0]
-        c0, width = span(k, half)
+        zz, y_ = (z, member) if along_y else (member, yy)
         if phase == 0:
-            return ref.at[zz, y_, :, pl.ds(c0, width)]
-        if half == 0:
-            return ref.at[zz, :, :, pl.ds(c0, width)]
-        return ref.at[:, y_, :, pl.ds(c0, width)]
-
-    def ring_copy(k, half, phase, d, arrival):
-        i = ((phase * 2 + half) * 4 + k) * 3 + d - 1
-        along_y = (half == 0) == (phase == 0)
-        if along_y:
-            dev = at(y_=y_peer[d])
+            ref = ref.at[zz, y_, :, pl.ds(c0, width)]
+        elif along_y:
+            ref = ref.at[:, y_, :, pl.ds(c0, width)]
         else:
-            dev = at(zz=z_peer[d])
-        zz, y_ = z, yy
-        if arrival:
-            if along_y:
-                y_ = y_peer[4 - d]
-            else:
-                zz = z_peer[4 - d]
-        ref = block(k, half, phase, zz, y_)
+            ref = ref.at[zz, :, :, pl.ds(c0, width)]
         return rdma(ref, ref, send_sem.at[i], recv_sem.at[i], dev)
+
+    def near(k, phase):
+        for half in (0, 1):
+            for link in (0, 1):
+                ring_copy(k, half, phase, link, False).start()
+
+    def relay_on(k, phase):
+        for half in (0, 1):
+            for link in (0, 1):
+                ring_copy(k, half, phase, link, True).wait_recv()
+                ring_copy(k, half, phase, link + 2, False).start()
+
+    def far_arrived(k, phase):
+        for half in (0, 1):
+            for link in (2, 3):
+                ring_copy(k, half, phase, link, True).wait_recv()
 
     own_main = pltpu.make_async_copy(main_ref, wall.at[z, yy, pl.ds(xh * 32, 32)], local_sem.at[0])
     own_rem = pltpu.make_async_copy(rem_ref, stag.at[z, yy, pl.ds(xh * 16, 16)], local_sem.at[1])
@@ -140,16 +156,26 @@
     for k in pieces:
         xh_copy(k).start()
 
+    lane = lax.broadcasted_iota(jnp.int32, (128, D), 1)
+    rest_lane = lane - MAIN
+    source = jnp.where(
+        lane < MAIN, (lane >> 5) * 36 + (lane & 31), (rest_lane >> 2) * 36 + 32 + (rest_lane & 3)
+    )
+    for i in range(9):
+        natural = lax.broadcasted_iota(jnp.int32, (128, D), 0) + i * 128
+        order[i * 128:(i + 1) * 128, :] = jnp.where(natural == source, 1.0, 0.0).astype(BF16)
+
     x_mine = x.at[:, pl.ds(col * 128, 128)]
+
+    def lat_copy():
+        return rdma(latp, x_mine, pass_send.at[4], pass_recv.at[4], col_dev)
 
     @pl.when(sec == 0)
     def _():
-        rdma(lat_ref, x_mine, pass_send.at[4], pass_recv.at[4], col_dev).start()
-        x[:, pl.ds(col * 128, 128), :] = lat_ref[...]
-
-    kbuf[...] = stale_k[...]
-    vbuf[...] = stale_v[...]
-    att[...] = jnp.zeros_like(att)
+        for j in range(4):
+            latp[j] = jnp.dot(lat_ref[place_ref[j]], order[...], preferred_element_type=F32).astype(BF16)
+        lat_copy().start()
+        x[:, pl.ds(col * 128, 128), :] = latp[...]
 
     own_cond.wait()
     rdma(
@@ -172,6 +198,17 @@
 
     for d in (1, 3, 2):
         cond_y(d, False).start()
+    own_main.wait()
+    own_rem.wait()
+
+    @pl.when(sec == 1)
+    def _():
+        pl.semaphore_wait(go_sem, 1)
+
+    xh_arrival(0).wait_recv()
+    near(0, 0)
+    xh_arrival(1).wait_recv()
+    near(1, 0)
     for d in (1, 3, 2):
         cond_y(d, True).wait_recv()
     for d in (1, 3, 2):
@@ -185,39 +222,45 @@
         part[i // 8, (i // 2) % 4, i % 2] = products[i:i + 1, :]
     for d in (1, 3, 2):
         part_z(d).start()
+    xh_arrival(2).wait_recv()
+    near(2, 0)
+    xh_arrival(3).wait_recv()
+    near(3, 0)
+    relay_on(0, 0)
+    relay_on(1, 0)
     for d in (1, 3, 2):
         part_z(d).wait_recv()
     sum_z[...] = part[z] + got_z[0] + got_z[1] + got_z[2]
     for d in (1, 3, 2):
         part_y(d).start()
+    far_arrived(0, 0)
+    near(0, 1)
+    relay_on(2, 0)
+    relay_on(3, 0)
     for d in (1, 3, 2):
         part_y(d).wait_recv()
     sum_y[...] = sum_z[yy] + got_y[0] + got_y[1] + got_y[2]
     part_x = rdma(sum_y.at[1 - xh], got_x, sum_send.at[6], sum_recv.at[6], xh_dev)
     part_x.start()
+    far_arrived(1, 0)
+    near(1, 1)
     part_x.wait_recv()
     mod_own[...] = sum_y[xh] + got_x[...]
     mod_copy = rdma(mod_own, mod_got, sum_send.at[7], sum_recv.at[7], col_dev)
     mod_copy.start()
-
-    own_main.wait()
-    own_rem.wait()
-    for k in pieces:
-        xh_arrival(k).wait_recv()
-        for half in (0, 1):
-            for d in (1, 3, 2):
-                ring_copy(k, half, 0, d, False).start()
-    for k in pieces:
-        for half in (0, 1):
-            for d in (1, 2, 3):
-                ring_copy(k, half, 0, d, True).wait_recv()
-            for d in (1, 3, 2):
-                ring_copy(k, half, 1, d, False).start()
-
-    def arrived(k):
-        for half in (0, 1):
-            for d in (1, 2, 3):
-                ring_copy(k, half, 1, d, True).wait_recv()
+    far_arrived(2, 0)
+    far_arrived(3, 0)
+    relay_on(0, 1)
+    near(2, 1)
+
+    for j in range(4):
+        kbuf[j, :, :576] = stale_k[place_ref[j]]
+        vbuf[j, :, :576] = stale_v[place_ref[j]]
+        kbuf[j, :, 576:] = jnp.zeros((256, HEADW - 576), BF16)
+        vbuf[j, :, 576:] = jnp.zeros((256, HEADW - 576), BF16)
+        token = lax.broadcasted_iota(jnp.int32, (1, 256), 1) + place_ref[j] * 256
+        valid_ref[:, j * 256:(j + 1) * 256] = jnp.where(token < length_ref[0], 1, 0)
+    att[...] = jnp.zeros_like(att)
 
     mod_copy.wait_recv()
     for k in range(6):
@@ -226,22 +269,22 @@
         mod_ref[k:k + 1, pl.ds((1 - col) * 512, 512)] = mod_got[:, base:base + 512]
         mod_ref[k:k + 1, MAIN:] = mod_own[:, base + 512:base + HEADW] + mod_got[:, base + 512:base + HEADW]
 
-    arrived(0)
+    relay_on(1, 1)
+    near(3, 1)
+    far_arrived(0, 1)
     rows_i = lax.broadcasted_iota(jnp.int32, (128, 512), 0)
     cols_i = lax.broadcasted_iota(jnp.int32, (128, 512), 1)
     for q in range(4):
         pick = jnp.where(
             ((cols_i >> 4) == (rows_i >> 2)) & ((cols_i & 15) == 4 * q + (rows_i & 3)), 1.0, 0.0
         ).astype(BF16)
-        for n in range(QUARTER // 256):
-            rest = stag[:, :, :, n * 256:(n + 1) * 256].reshape(512, 256)
-            wrem[:, q * QUARTER + n * 256:q * QUARTER + (n + 1) * 256] = jnp.dot(
-                pick, rest, preferred_element_type=F32
-            ).astype(BF16)
+        wrem[:, q * QUARTER:(q + 1) * QUARTER] = jnp.dot(
+            pick, stag[...].reshape(512, QUARTER), preferred_element_type=F32
+        ).astype(BF16)
 
     def norm_rows(load, shift, scale):
         def body(i, carry):
-            rows = pl.ds(pl.multiple_of(i * 32, 32), 32)
+            rows = pl.ds(pl.multiple_of(i * 64, 64), 64)
             v = load(rows)
             mean = jnp.sum(v, axis=-1, keepdims=True) * (1.0 / D)
             v = v - mean
@@ -249,7 +292,7 @@
             normed = v * lax.rsqrt(var + 1e-6)
             h[rows, :] = (normed * (1.0 + scale[...]) + shift[...]).astype(BF16)
             return carry
-        lax.fori_loop(0, 8, body, 0)
+        lax.fori_loop(0, 4, body, 0, unroll=4)
 
     def times(lhs_ref, c0, width):
         return jnp.dot(
@@ -257,13 +300,9 @@
         ) + jnp.dot(lhs_ref[:, MAIN:], wrem[:, pl.ds(c0, width)], preferred_element_type=F32)
 
     def times_t(load, dst, j, c0, width):
-        def body(zz, carry):
-            w = wall[zz, :, :, pl.ds(c0, width)].reshape(256, width)
-            dst[j, :, pl.ds(pl.multiple_of(zz * 256, 256), 256)] = lax.dot_general(
-                load(), w, NT, preferred_element_type=F32
-            ).astype(BF16)
-            return carry
-        lax.fori_loop(0, 4, body, 0)
+        dst[j, :, :MAIN] = lax.dot_general(
+            load(), wall[:, :, :, pl.ds(c0, width)].reshape(MAIN, width), NT, preferred_element_type=F32
+        ).astype(BF16)
         dst[j, :, MAIN:] = lax.dot_general(
             load(), wrem[:, pl.ds(c0, width)], NT, preferred_element_type=F32
         ).astype(BF16)
@@ -274,14 +313,28 @@
     def pass_copy(j):
         return rdma(y.at[j], x.at[j], pass_send.at[j], pass_recv.at[j], sec_dev)
 
-    arrived(1)
+    def half_copy(j):
+        part_rows = pl.ds((1 - col) * 128, 128)
+        return rdma(
+            pm_own.at[j, part_rows], pm_got.at[j, part_rows], col_send.at[4 + j], col_recv.at[4 + j], col_dev
+        )
+
+    def mlp_copy(j, act):
+        @pl.when(sec == 0)
+        def _():
+            act(col_copy(pm_own, pm_got, j, 4))
+
+        @pl.when(sec == 1)
+        def _():
+            act(half_copy(j))
+
+    far_arrived(1, 1)
 
     @pl.when(sec == 0)
     def _():
-        x_theirs = x.at[:, pl.ds((1 - col) * 128, 128)]
-        rdma(lat_ref, x_theirs, pass_send.at[4], pass_recv.at[4], col_dev).wait_recv()
-
-    def attend_step(j, carry):
+        lat_copy().wait_recv()
+
+    def attend_step(j):
         @pl.when(sec == 1)
         def _():
             pass_copy(j).wait_recv()
@@ -310,15 +363,11 @@
                 mixed = jnp.where(mine, got / totals, mixed)
             att[:, window] = mixed.astype(BF16)
             return c
-        lax.fori_loop(0, 4, heads, 0)
+        lax.fori_loop(0, 4, heads, 0, unroll=2)
         times_t(lambda: att[...], pa_own, j, COL_OUT, HEADW)
         col_copy(pa_own, pa_got, j, 0).start()
-        return carry
-    lax.fori_loop(0, 4, attend_step, 0)
-
-    arrived(2)
-
-    def up_step(j, carry):
+
+    def mlp_step(j):
         col_copy(pa_own, pa_got, j, 0).wait_recv()
 
         def load(rows):
@@ -330,43 +379,67 @@
         norm_rows(load, mod_ref.at[3:4], mod_ref.at[4:5])
 
         def body(n, c):
-            u = times(h, pl.multiple_of(COL_UP + n * 256, 256), 256)
+            u = times(h, pl.multiple_of(COL_UP + n * 768, 256), 768)
             g = 0.5 * u * (1.0 + jnp.tanh(math.sqrt(2.0 / math.pi) * (u + 0.044715 * (u * u * u))))
-            hid[j, :, pl.ds(pl.multiple_of(n * 256, 256), 256)] = g.astype(BF16)
+            hid[:, pl.ds(pl.multiple_of(n * 768, 256), 768)] = g.astype(BF16)
             return c
-        lax.fori_loop(0, 9, body, 0)
-        return carry
-    lax.fori_loop(0, 4, up_step, 0)
-
-    arrived(3)
+        lax.fori_loop(0, 3, body, 0)
+        times_t(lambda: hid[...], pm_own, j, COL_DOWN, 2304)
+        mlp_copy(j, lambda copy: copy.start())
 
     def finish(j):
-        col_copy(pm_own, pm_got, j, 4).wait_recv()
-
-        def body(i, c):
-            rows = pl.ds(pl.multiple_of(i * 32, 32), 32)
+        mlp_copy(j, lambda copy: copy.wait_recv())
+
+        def settle(i):
+            rows = pl.ds(pl.multiple_of(i * 64, 64), 64)
             y[j, rows, :] = (
                 x1[j, rows, :]
                 + mod_ref[5:6] * (pm_own[j, rows, :].astype(F32) + pm_got[j, rows, :].astype(F32))
             ).astype(BF16)
-            return c
-        lax.fori_loop(0, 8, body, 0)
 
         @pl.when(sec == 0)
         def _():
+            lax.fori_loop(0, 4, lambda i, c: settle(i) or c, 0)
             pass_copy(j).start()
-        out_ref[j] = y[j, pl.ds(col * 128, 128), :]
-
-    def down_step(j, carry):
-        times_t(lambda: hid[j], pm_own, j, COL_DOWN, 2304)
-        col_copy(pm_own, pm_got, j, 4).start()
-
-        @pl.when(j > 0)
-        def _():
-            finish(j - 1)
+
+        @pl.when(sec == 1)
+        def _():
+            lax.fori_loop(0, 2, lambda i, c: settle(col * 2 + i) or c, 0)
+        yout[j] = lax.dot_general(
+            y[j, pl.ds(col * 128, 128), :], order[...], NT, preferred_element_type=F32
+        ).astype(BF16)
+
+    def step(t, carry):
+        @pl.when(t < 4)
+        def _():
+            attend_step(t)
+
+        @pl.when(t == 0)
+        def _():
+            relay_on(2, 1)
+
+            @pl.when(sec == 0)
+            def _():
+                pl.semaphore_signal(go_sem, inc=1, device_id=sec_dev, device_id_type=MESH)
+
+        @pl.when(t == 1)
+        def _():
+            relay_on(3, 1)
+            far_arrived(2, 1)
+            far_arrived(3, 1)
+
+        @pl.when(t > 1)
+        def _():
+            finish(t - 2)
+
+        @pl.when(t > 0)
+        def _():
+            mlp_step(t - 1)
         return carry
-    lax.fori_loop(0, 4, down_step, 0)
+    lax.fori_loop(0, 5, step, 0)
     finish(3)
+    for p in range(4):
+        out_ref[p] = yout[slot_ref[p]]
 
     cond_xh.wait_send()
     for d in (1, 2, 3):
@@ -380,12 +453,12 @@
         xh_copy(k).wait_send()
         for phase in (0, 1):
             for half in (0, 1):
-                for d in (1, 2, 3):
-                    ring_copy(k, half, phase, d, False).wait_send()
+                for link in range(4):
+                    ring_copy(k, half, phase, link, False).wait_send()
 
     def drain(j, c):
         col_copy(pa_own, pa_got, j, 0).wait_send()
-        col_copy(pm_own, pm_got, j, 4).wait_send()
+        mlp_copy(j, lambda copy: copy.wait_send())
 
         @pl.when(sec == 0)
         def _():
@@ -395,18 +468,22 @@
 
     @pl.when(sec == 0)
     def _():
-        rdma(lat_ref, x_mine, pass_send.at[4], pass_recv.at[4], col_dev).wait_send()
-
-
-def run_relay(valid, cond, ada, lat, stale_k, stale_v, main, rem):
+        lat_copy().wait_send()
+
+
+def run_relay(place, slot, length, cond, ada, lat, stale_k, stale_v, main, rem):
     vmem = pl.BlockSpec(memory_space=pltpu.VMEM)
     tokens = (4, 256, D)
     return pl.pallas_call(
         relay,
         out_shape=jax.ShapeDtypeStruct((4, 128, D), BF16),
-        in_specs=[vmem] * 8,
+        in_specs=[pl.BlockSpec(memory_space=pltpu.SMEM)] * 3 + [vmem] * 7,
         out_specs=vmem,
         scratch_shapes=[
+            pltpu.VMEM((D, D), BF16),
+            pltpu.VMEM((1, 1024), jnp.int32),
+            pltpu.VMEM((4, 128, D), BF16),
+            pltpu.VMEM((4, 128, D), BF16),
             pltpu.VMEM((4, 4, 64, 128), F32),
             pltpu.VMEM((32, 128), F32),
             pltpu.VMEM((4, 4, 2, 1, MODW), F32),
@@ -427,7 +504,7 @@
             pltpu.VMEM((4, 256, HEADW), BF16),
             pltpu.VMEM((4, 256, HEADW), BF16),
             pltpu.VMEM((256, HEADW), BF16),
-            pltpu.VMEM((4, 256, 2304), BF16),
+            pltpu.VMEM((256, 2304), BF16),
             pltpu.VMEM((256, D), BF16),
             pltpu.VMEM(tokens, BF16),
             pltpu.VMEM(tokens, BF16),
@@ -438,11 +515,12 @@
             pltpu.SemaphoreType.DMA((7,)),
             pltpu.SemaphoreType.DMA((8,)),
             pltpu.SemaphoreType.DMA((8,)),
+            pltpu.SemaphoreType.REGULAR,
             pltpu.SemaphoreType.DMA((3,)),
             pltpu.SemaphoreType.DMA((4,)),
             pltpu.SemaphoreType.DMA((4,)),
-            pltpu.SemaphoreType.DMA((48,)),
-            pltpu.SemaphoreType.DMA((48,)),
+            pltpu.SemaphoreType.DMA((64,)),
+            pltpu.SemaphoreType.DMA((64,)),
             pltpu.SemaphoreType.DMA((8,)),
             pltpu.SemaphoreType.DMA((8,)),
             pltpu.SemaphoreType.DMA((5,)),
@@ -451,7 +529,7 @@
         compiler_params=pltpu.CompilerParams(
             collective_id=0, has_side_effects=True, vmem_limit_bytes=67043328
         ),
-    )(valid, cond, ada, lat, stale_k, stale_v, main, rem)
+    )(place, slot, length, cond, ada, lat, stale_k, stale_v, main, rem)
 
 
 def local(
@@ -478,13 +556,6 @@
     ada = jnp.einsum("dkc,ce->dke", ada_weight[0], spread, preferred_element_type=F32).astype(BF16)
     ada = jnp.pad(ada.reshape(36, MODW), ((0, 92), (0, 0)))
 
-    place = jnp.arange(D, dtype=jnp.int32)
-    rest = place - MAIN
-    source = jnp.where(place < MAIN, (place // 32) * 36 + place % 32, (rest // 4) * 36 + 32 + rest % 4)
-    order = (place[:, None] == source[None, :]).astype(BF16)
-    lat = jnp.take(latents[0], patch_order, axis=0)
-    lat = jnp.einsum("ptd,de->pte", lat, order, preferred_element_type=F32).astype(BF16)
-
     pad = lambda a, n: jnp.pad(a, ((0, 0), (0, n - a.shape[1])))
     shard = jnp.concatenate(
         [pad(qkv_weight[0, :, i], HEADW) for i in range(3)]
@@ -494,14 +565,11 @@
     main = shard[:32]
     rem = shard[32:].reshape(4, 4, QUARTER).transpose(1, 0, 2).reshape(16, QUARTER)
 
-    wide = lambda a: jnp.pad(jnp.take(a, patch_order, axis=0), ((0, 0), (0, 0), (0, HEADW - a.shape[2])))
-    position = patch_order[:, None] * 256 + jnp.arange(256, dtype=jnp.int32)[None, :]
-    valid = (position < lengths[0]).astype(jnp.int32).reshape(1, 1024)
-
-    out = run_relay(valid, cond, ada, lat, wide(stale_keys[0, 0]), wide(stale_values[0, 0]), main, rem)
-    out = jnp.einsum("pte,de->ptd", out, order, preferred_element_type=F32).astype(BF16)
-    where = jnp.argmax(patch_order[None, :] == jnp.arange(4, dtype=jnp.int32)[:, None], axis=1)
-    return jnp.take(out, where, axis=0)[None, None]
+    slot = jnp.argmax(patch_order[None, :] == jnp.arange(4, dtype=jnp.int32)[:, None], axis=1).astype(jnp.int32)
+    out = run_relay(
+        patch_order, slot, lengths, cond, ada, latents[0], stale_keys[0, 0], stale_values[0, 0], main, rem
+    )
+    return out[None, None]
 
 
 def solution(mesh):

time: 300 us -> 201 us (0.67)
  Pallas kernels: 270 us -> 186 us
  matrix products: 6.7 us -> 1.55 us
  local copies, waits for them, and re-layouts: 14.7 us -> 9.68 us
  other arithmetic: 6.32 us -> 2.16 us
    pallas_call x1, Pallas kernels: 270 us -> 186 us  [run_relay(): pl.pallas_call(relay, out_shape=jax.ShapeDtypeStruct((4, 128, D), BF16),...]
    gather x6 -> x0, local copies, waits for them, and re-layouts: 7.54 us -> none  [the longest x4 5.96 us: local(): jnp.take(a, patch_order, axis=0)]
    dot_general x2 -> x0, matrix products: 6.11 us -> none  [the longest x1 3.16 us: local(): jnp.einsum('pte,de->ptd', out, order, preferred_element_type=F32)]
    unnamed x28 -> x20, local copies, waits for them, and re-layouts: 2.1 us -> 6.21 us
where the time goes in v3:
time: 201 us
  Pallas kernels  186 us (93%)
  local copies, waits for them, and re-layouts  9.68 us (5%)
  other arithmetic  2.16 us (1%)
    pallas_call x1, Pallas kernels, run_relay(): pl.pallas_call(relay, out_shape=jax.ShapeDtypeStruct((4, 128, D), BF16),...  186 us
    unnamed x20, local copies, waits for them, and re-layouts  6.21 us

profile of v3, /device:TPU:1, one launch (start us, length us, event | category | flops | bytes accessed | tf_op | source)
XLA Modules:
  0.0 201.2 jit_solution(1244013731465674915)
XLA Ops:
  1.3 1.3 iota_reduce_fusion
  2.6 0.1 fusion.17
  2.8 0.1 maximum_reduce_fusion
  2.8 0.1 concatenate.13
  3.0 0.6 pad_convert_fusion.cond_ref
  3.6 0.9 slice_bitcast_fusion
  4.5 1.6 fusion.6
  6.0 0.0 copy-start.4
  6.0 0.0 copy-start.2
  6.1 0.0 copy-start.3
  6.1 0.1 pad.32
  6.3 0.5 copy-done.4
  6.8 0.1 copy-done.2
  7.0 0.1 copy-done.3
  7.1 0.0 copy-start
  7.1 0.8 slice.20.main_ref
  7.9 0.6 reshape.77.rem_ref
  8.5 1.0 pad.25.ada_ref
  9.6 0.0 copy-done
  9.6 0.0 copy-start.1
  9.6 1.4 copy.21
  11.0 0.0 copy-done.1
  11.0 1.4 copy.22
  12.4 186.3 %shard_map.109 = bf16[4,128,1152]{2,1,0:T(8,128)(2,1)} custom-call(s32[4]{0:T(128)} %place_ref.1, s32[4]{0:T(128)} %get-tuple-element.6.slot_ref, s32[1]{0:T(128)S(6)} %copy.32.length_ref, f32[32,128]{1,0:T(8,128)} %pad_convert_fusion.cond_ref, bf16[128,3840]{1,0:T(8,128)(2,1)} %pad.25.ada_ref, bf16[4,128,1152]{2,1,0:T(8,128)(2,1)} %bitcast.43, ...), custom_call_target="tpu_custom_call" | custom-call | tf_op jit(solution)/shard_map/pallas_call | solution.py:477
  198.8 2.4 %copy.33 = bf16[1,1,4,128,1152]{4,3,2,1,0:T(8,128)(2,1)} copy(bf16[1,1,4,128,1152]{4,3,2,1,0:T(8,128)(2,1)} %bitcast.40) | data formatting | bytes 2359296
  (11 shorter events, 0.2 us)
Async XLA Ops:
  6.0 0.8 copy-start.4
  6.0 0.9 copy-start.2
  6.1 1.0 copy-start.3
  7.1 2.4 %copy-start = (bf16[1,1,4,256,576]{3,4,2,1,0:T(8,128)(2,1)S(1)}, bf16[1,1,4,256,576]{3,4,2,1,0:T(8,128)(2,1)}, u32[]{:S(2)}) copy-start(bf16[1,1,4,256,576]{3,4,2,1,0:T(8,128)(2,1)} %param.20) | copy-start | bytes 3538948
  9.6 1.5 copy-start.1

commit v4 on v3

--- a/solution.py
+++ b/solution.py
@@ -39,8 +39,8 @@
 
 
 def relay(
-    place_ref, slot_ref, length_ref, cond_ref, ada_ref, lat_ref, stale_k, stale_v, main_ref, rem_ref, out_ref,
-    order, valid_ref, latp, yout,
+    place_ref, length_ref, cond_ref, ada_ref, lat_ref, keys_ref, values_ref, main_ref, rem_ref, out_ref,
+    order, mask_ref, stale_k, stale_v, latp, yout,
     cbuf, cmat, part, got_z, sum_z, got_y, sum_y, got_x, mod_own, mod_got, mod_ref,
     wall, stag, wrem, x, x1, qs, kbuf, vbuf, att, hid, h, pa_own, pa_got, pm_own, pm_got, y,
     cond_send, cond_recv, sum_send, sum_recv, go_sem, local_sem, xh_send, xh_recv, send_sem, recv_sem, col_send, col_recv, pass_send, pass_recv,
@@ -145,37 +145,46 @@
             for link in (2, 3):
                 ring_copy(k, half, phase, link, True).wait_recv()
 
+    def go():
+        @pl.when(sec == 0)
+        def _():
+            pl.semaphore_signal(go_sem, inc=1, device_id=sec_dev, device_id_type=MESH)
+
+    def await_go():
+        @pl.when(sec == 1)
+        def _():
+            pl.semaphore_wait(go_sem, 1)
+
+    own_keys = pltpu.make_async_copy(keys_ref, stale_k, local_sem.at[3])
+    own_values = pltpu.make_async_copy(values_ref, stale_v, local_sem.at[4])
     own_main = pltpu.make_async_copy(main_ref, wall.at[z, yy, pl.ds(xh * 32, 32)], local_sem.at[0])
     own_rem = pltpu.make_async_copy(rem_ref, stag.at[z, yy, pl.ds(xh * 16, 16)], local_sem.at[1])
     own_cond = pltpu.make_async_copy(cond_ref, cbuf.at[z, yy, pl.ds(xh * 32, 32)], local_sem.at[2])
+    cond_xh = rdma(cond_ref, cbuf.at[z, yy, pl.ds(xh * 32, 32)], cond_send.at[0], cond_recv.at[0], xh_dev)
     own_cond.start()
-    cond_xh = rdma(cond_ref, cbuf.at[z, yy, pl.ds(xh * 32, 32)], cond_send.at[0], cond_recv.at[0], xh_dev)
-    cond_xh.start()
     own_main.start()
     own_rem.start()
+    own_keys.start()
+    own_values.start()
+    await_go()
+    cond_xh.start()
     for k in pieces:
         xh_copy(k).start()
 
-    lane = lax.broadcasted_iota(jnp.int32, (128, D), 1)
-    rest_lane = lane - MAIN
-    source = jnp.where(
-        lane < MAIN, (lane >> 5) * 36 + (lane & 31), (rest_lane >> 2) * 36 + 32 + (rest_lane & 3)
-    )
-    for i in range(9):
-        natural = lax.broadcasted_iota(jnp.int32, (128, D), 0) + i * 128
-        order[i * 128:(i + 1) * 128, :] = jnp.where(natural == source, 1.0, 0.0).astype(BF16)
+    def build_order():
+        lane = lax.broadcasted_iota(jnp.int32, (128, D), 1)
+        rest_lane = lane - MAIN
+        source = jnp.where(
+            lane < MAIN, (lane >> 5) * 36 + (lane & 31), (rest_lane >> 2) * 36 + 32 + (rest_lane & 3)
+        )
+        for i in range(9):
+            natural = lax.broadcasted_iota(jnp.int32, (128, D), 0) + i * 128
+            order[i * 128:(i + 1) * 128, :] = jnp.where(natural == source, 1.0, 0.0).astype(BF16)
 
     x_mine = x.at[:, pl.ds(col * 128, 128)]
 
     def lat_copy():
         return rdma(latp, x_mine, pass_send.at[4], pass_recv.at[4], col_dev)
-
-    @pl.when(sec == 0)
-    def _():
-        for j in range(4):
-            latp[j] = jnp.dot(lat_ref[place_ref[j]], order[...], preferred_element_type=F32).astype(BF16)
-        lat_copy().start()
-        x[:, pl.ds(col * 128, 128), :] = latp[...]
 
     own_cond.wait()
     rdma(
@@ -198,21 +207,11 @@
 
     for d in (1, 3, 2):
         cond_y(d, False).start()
-    own_main.wait()
-    own_rem.wait()
-
-    @pl.when(sec == 1)
-    def _():
-        pl.semaphore_wait(go_sem, 1)
-
-    xh_arrival(0).wait_recv()
-    near(0, 0)
-    xh_arrival(1).wait_recv()
-    near(1, 0)
     for d in (1, 3, 2):
         cond_y(d, True).wait_recv()
     for d in (1, 3, 2):
         cond_z(d, False).start()
+    build_order()
     for d in (1, 3, 2):
         cond_z(d, True).wait_recv()
     for i in range(32):
@@ -222,26 +221,40 @@
         part[i // 8, (i // 2) % 4, i % 2] = products[i:i + 1, :]
     for d in (1, 3, 2):
         part_z(d).start()
-    xh_arrival(2).wait_recv()
-    near(2, 0)
-    xh_arrival(3).wait_recv()
-    near(3, 0)
-    relay_on(0, 0)
-    relay_on(1, 0)
+
+    @pl.when(sec == 0)
+    def _():
+        for j in range(4):
+            latp[j] = jnp.dot(lat_ref[place_ref[j]], order[...], preferred_element_type=F32).astype(BF16)
+
+    own_main.wait()
+    own_rem.wait()
+    await_go()
+    for k in pieces:
+        xh_arrival(k).wait_recv()
+        near(k, 0)
+    go()
+
+    @pl.when(sec == 0)
+    def _():
+        lat_copy().start()
+        x[:, pl.ds(col * 128, 128), :] = latp[...]
+
     for d in (1, 3, 2):
         part_z(d).wait_recv()
     sum_z[...] = part[z] + got_z[0] + got_z[1] + got_z[2]
     for d in (1, 3, 2):
         part_y(d).start()
-    far_arrived(0, 0)
-    near(0, 1)
-    relay_on(2, 0)
-    relay_on(3, 0)
+    for k in pieces:
+        relay_on(k, 0)
     for d in (1, 3, 2):
         part_y(d).wait_recv()
     sum_y[...] = sum_z[yy] + got_y[0] + got_y[1] + got_y[2]
     part_x = rdma(sum_y.at[1 - xh], got_x, sum_send.at[6], sum_recv.at[6], xh_dev)
     part_x.start()
+    await_go()
+    far_arrived(0, 0)
+    near(0, 1)
     far_arrived(1, 0)
     near(1, 1)
     part_x.wait_recv()
@@ -253,13 +266,15 @@
     relay_on(0, 1)
     near(2, 1)
 
+    own_keys.wait()
+    own_values.wait()
     for j in range(4):
         kbuf[j, :, :576] = stale_k[place_ref[j]]
         vbuf[j, :, :576] = stale_v[place_ref[j]]
         kbuf[j, :, 576:] = jnp.zeros((256, HEADW - 576), BF16)
         vbuf[j, :, 576:] = jnp.zeros((256, HEADW - 576), BF16)
         token = lax.broadcasted_iota(jnp.int32, (1, 256), 1) + place_ref[j] * 256
-        valid_ref[:, j * 256:(j + 1) * 256] = jnp.where(token < length_ref[0], 1, 0)
+        mask_ref[:, j * 256:(j + 1) * 256] = jnp.where(token < length_ref[0], 0.0, -1e30)
     att[...] = jnp.zeros_like(att)
 
     mod_copy.wait_recv()
@@ -271,6 +286,7 @@
 
     relay_on(1, 1)
     near(3, 1)
+    go()
     far_arrived(0, 1)
     rows_i = lax.broadcasted_iota(jnp.int32, (128, 512), 0)
     cols_i = lax.broadcasted_iota(jnp.int32, (128, 512), 1)
@@ -340,9 +356,10 @@
             pass_copy(j).wait_recv()
 
         norm_rows(lambda rows: x[j, rows, :].astype(F32), mod_ref.at[0:1], mod_ref.at[1:2])
-        qs[...] = times(h, 0, HEADW).astype(BF16)
-        kbuf[j] = times(h, HEADW, HEADW).astype(BF16)
-        vbuf[j] = times(h, 2 * HEADW, HEADW).astype(BF16)
+        qkv = times(h, 0, 3 * HEADW).astype(BF16)
+        qs[...] = qkv[:, :HEADW]
+        kbuf[j] = qkv[:, HEADW:2 * HEADW]
+        vbuf[j] = qkv[:, 2 * HEADW:]
 
         def heads(p, c):
             window = pl.ds(pl.multiple_of(p * 128, 128), 256)
@@ -355,15 +372,14 @@
                 mine = (lane >= e * HD) & (lane < (e + 1) * HD)
                 scores = lax.dot_general(
                     jnp.where(mine, q_win.astype(F32), 0.0).astype(BF16), k_win, NT, preferred_element_type=F32
-                ) * (1.0 / math.sqrt(HD))
-                scores = jnp.where(valid_ref[...] > 0, scores, -1e30)
-                weights = jnp.exp(scores - jnp.max(scores, axis=-1, keepdims=True))
+                ) * (math.log2(math.e) / math.sqrt(HD)) + mask_ref[...]
+                weights = jnp.exp2(scores - jnp.max(scores, axis=-1, keepdims=True))
                 totals = jnp.sum(weights, axis=-1, keepdims=True)
                 got = jnp.dot(weights.astype(BF16), v_win, preferred_element_type=F32)
-                mixed = jnp.where(mine, got / totals, mixed)
+                mixed = jnp.where(mine, got * (1.0 / totals), mixed)
             att[:, window] = mixed.astype(BF16)
             return c
-        lax.fori_loop(0, 4, heads, 0, unroll=2)
+        lax.fori_loop(0, 4, heads, 0, unroll=4)
         times_t(lambda: att[...], pa_own, j, COL_OUT, HEADW)
         col_copy(pa_own, pa_got, j, 0).start()
 
@@ -383,7 +399,7 @@
             g = 0.5 * u * (1.0 + jnp.tanh(math.sqrt(2.0 / math.pi) * (u + 0.044715 * (u * u * u))))
             hid[:, pl.ds(pl.multiple_of(n * 768, 256), 768)] = g.astype(BF16)
             return c
-        lax.fori_loop(0, 3, body, 0)
+        lax.fori_loop(0, 3, body, 0, unroll=3)
         times_t(lambda: hid[...], pm_own, j, COL_DOWN, 2304)
         mlp_copy(j, lambda copy: copy.start())
 
@@ -417,14 +433,11 @@
         @pl.when(t == 0)
         def _():
             relay_on(2, 1)
-
-            @pl.when(sec == 0)
-            def _():
-                pl.semaphore_signal(go_sem, inc=1, device_id=sec_dev, device_id_type=MESH)
+            relay_on(3, 1)
+            go()
 
         @pl.when(t == 1)
         def _():
-            relay_on(3, 1)
             far_arrived(2, 1)
             far_arrived(3, 1)
 
@@ -439,7 +452,10 @@
     lax.fori_loop(0, 5, step, 0)
     finish(3)
     for p in range(4):
-        out_ref[p] = yout[slot_ref[p]]
+        slot = jnp.int32(0)
+        for j in range(1, 4):
+            slot = jnp.where(place_ref[j] == p, j, slot)
+        out_ref[p] = yout[slot]
 
     cond_xh.wait_send()
     for d in (1, 2, 3):
@@ -471,17 +487,19 @@
         lat_copy().wait_send()
 
 
-def run_relay(place, slot, length, cond, ada, lat, stale_k, stale_v, main, rem):
+def run_relay(place, length, cond, ada, lat, stale_k, stale_v, main, rem):
     vmem = pl.BlockSpec(memory_space=pltpu.VMEM)
     tokens = (4, 256, D)
     return pl.pallas_call(
         relay,
         out_shape=jax.ShapeDtypeStruct((4, 128, D), BF16),
-        in_specs=[pl.BlockSpec(memory_space=pltpu.SMEM)] * 3 + [vmem] * 7,
+        in_specs=[pl.BlockSpec(memory_space=pltpu.SMEM)] * 2 + [vmem] * 3 + [pl.BlockSpec(memory_space=pl.ANY)] * 2 + [vmem] * 2,
         out_specs=vmem,
         scratch_shapes=[
             pltpu.VMEM((D, D), BF16),
-            pltpu.VMEM((1, 1024), jnp.int32),
+            pltpu.VMEM((1, 1024), F32),
+            pltpu.VMEM((4, 256, 576), BF16),
+            pltpu.VMEM((4, 256, 576), BF16),
             pltpu.VMEM((4, 128, D), BF16),
             pltpu.VMEM((4, 128, D), BF16),
             pltpu.VMEM((4, 4, 64, 128), F32),
@@ -516,7 +534,7 @@
             pltpu.SemaphoreType.DMA((8,)),
             pltpu.SemaphoreType.DMA((8,)),
             pltpu.SemaphoreType.REGULAR,
-            pltpu.SemaphoreType.DMA((3,)),
+            pltpu.SemaphoreType.DMA((5,)),
             pltpu.SemaphoreType.DMA((4,)),
             pltpu.SemaphoreType.DMA((4,)),
             pltpu.SemaphoreType.DMA((64,)),
@@ -529,7 +547,7 @@
         compiler_params=pltpu.CompilerParams(
             collective_id=0, has_side_effects=True, vmem_limit_bytes=67043328
         ),
-    )(place, slot, length, cond, ada, lat, stale_k, stale_v, main, rem)
+    )(place, length, cond, ada, lat, stale_k, stale_v, main, rem)
 
 
 def local(
@@ -565,9 +583,8 @@
     main = shard[:32]
     rem = shard[32:].reshape(4, 4, QUARTER).transpose(1, 0, 2).reshape(16, QUARTER)
 
-    slot = jnp.argmax(patch_order[None, :] == jnp.arange(4, dtype=jnp.int32)[:, None], axis=1).astype(jnp.int32)
     out = run_relay(
-        patch_order, slot, lengths, cond, ada, latents[0], stale_keys[0, 0], stale_values[0, 0], main, rem
+        patch_order, lengths, cond, ada, latents[0], stale_keys[0, 0], stale_values[0, 0], main, rem
     )
     return out[None, None]
 

time: 201 us -> 209 us (1.040)
  Pallas kernels: 186 us -> 195 us
    pallas_call x1, Pallas kernels: 186 us -> 195 us  [run_relay(): pl.pallas_call(relay, out_shape=jax.ShapeDtypeStruct((4, 128, D), BF16),...]
where the time goes in v4:
time: 209 us
  Pallas kernels  195 us (93%)
  local copies, waits for them, and re-layouts  9.65 us (5%)
    pallas_call x1, Pallas kernels, run_relay(): pl.pallas_call(relay, out_shape=jax.ShapeDtypeStruct((4, 128, D), BF16),...  195 us
    unnamed x20, local copies, waits for them, and re-layouts  6.18 us

profile of v4, /device:TPU:1, one launch (start us, length us, event | category | flops | bytes accessed | tf_op | source)
XLA Modules:
  0.0 208.5 jit_solution(18277754954796361525)
XLA Ops:
  1.3 0.1 fusion.17
  1.4 0.1 maximum_reduce_fusion
  1.5 0.1 concatenate.13
  1.6 0.6 pad_convert_fusion.cond_ref
  2.2 0.9 slice_bitcast_fusion
  3.1 1.6 fusion.6
  4.7 0.0 copy-start.4
  4.7 0.0 copy-start.2
  4.8 0.0 copy-start.3
  4.8 0.1 pad.32
  4.9 0.5 copy-done.4
  5.5 0.1 copy-done.2
  5.6 0.1 copy-done.3
  5.8 0.0 copy-start
  5.8 0.8 slice.20.main_ref
  6.6 0.6 reshape.76.rem_ref
  7.2 1.0 pad.25.ada_ref
  8.2 0.0 copy-done
  8.2 0.0 copy-start.1
  8.2 1.4 copy.17
  9.7 0.0 copy-done.1
  9.7 1.4 copy.18
  11.1 195.0 %shard_map.109 = bf16[4,128,1152]{2,1,0:T(8,128)(2,1)} custom-call(s32[4]{0:T(128)} %place_ref.1, s32[1]{0:T(128)S(6)} %copy.28.length_ref, f32[32,128]{1,0:T(8,128)} %pad_convert_fusion.cond_ref, bf16[128,3840]{1,0:T(8,128)(2,1)} %pad.25.ada_ref, bf16[4,128,1152]{2,1,0:T(8,128)(2,1)} %bitcast.43, bf16[4,256,576]{2,1,0:T(8,128)(2,1)} %bitcast.38, ...), custom_call_target="tpu_custom_call" | custom-call | tf_op jit(solution)/shard_map/pallas_call | solution.py:493
  206.1 2.4 %copy.29 = bf16[1,1,4,128,1152]{4,3,2,1,0:T(8,128)(2,1)} copy(bf16[1,1,4,128,1152]{4,3,2,1,0:T(8,128)(2,1)} %bitcast.40) | data formatting | bytes 2359296
  (11 shorter events, 0.2 us)
Async XLA Ops:
  4.7 0.8 copy-start.4
  4.7 0.9 copy-start.2
  4.8 1.0 copy-start.3
  5.8 2.5 %copy-start = (bf16[1,1,4,256,576]{3,4,2,1,0:T(8,128)(2,1)S(1)}, bf16[1,1,4,256,576]{3,4,2,1,0:T(8,128)(2,1)}, u32[]{:S(2)}) copy-start(bf16[1,1,4,256,576]{3,4,2,1,0:T(8,128)(2,1)} %param.20) | copy-start | bytes 3538948
  8.2 1.4 copy-start.1

commit v5 on v4

--- a/solution.py
+++ b/solution.py
@@ -19,6 +19,7 @@
 COLS = COL_DOWN + 2304
 QUARTER = COLS // 4
 MODW = 6 * HEADW
+ADAROWS = 48
 CHUNKS = ((0, COL_UP), (COL_UP, COL_DOWN), (COL_DOWN, COLS))
 MAIN = 1024
 MESH = pl.DeviceIdType.MESH
@@ -41,9 +42,9 @@
 def relay(
     place_ref, length_ref, cond_ref, ada_ref, lat_ref, keys_ref, values_ref, main_ref, rem_ref, out_ref,
     order, mask_ref, stale_k, stale_v, latp, yout,
-    cbuf, cmat, part, got_z, sum_z, got_y, sum_y, got_x, mod_own, mod_got, mod_ref,
+    cbuf, cmat, ada_got, part, got_z, sum_z, got_y, sum_y, got_x, mods, mod_ref,
     wall, stag, wrem, x, x1, qs, kbuf, vbuf, att, hid, h, pa_own, pa_got, pm_own, pm_got, y,
-    cond_send, cond_recv, sum_send, sum_recv, go_sem, local_sem, xh_send, xh_recv, send_sem, recv_sem, col_send, col_recv, pass_send, pass_recv,
+    give_send, give_recv, cond_send, cond_recv, sum_send, sum_recv, go_sem, local_sem, xh_send, xh_recv, send_sem, recv_sem, col_send, col_recv, pass_send, pass_recv,
 ):
     sec = lax.axis_index("section")
     row = lax.axis_index("row")
@@ -161,15 +162,17 @@
     own_rem = pltpu.make_async_copy(rem_ref, stag.at[z, yy, pl.ds(xh * 16, 16)], local_sem.at[1])
     own_cond = pltpu.make_async_copy(cond_ref, cbuf.at[z, yy, pl.ds(xh * 32, 32)], local_sem.at[2])
     cond_xh = rdma(cond_ref, cbuf.at[z, yy, pl.ds(xh * 32, 32)], cond_send.at[0], cond_recv.at[0], xh_dev)
-    own_cond.start()
     own_main.start()
     own_rem.start()
     own_keys.start()
     own_values.start()
-    await_go()
-    cond_xh.start()
-    for k in pieces:
-        xh_copy(k).start()
+    ada_copy = rdma(ada_ref, ada_got, give_send.at[0], give_recv.at[0], sec_dev)
+    mods_0 = mods.at[:, :, pl.ds(0, MODW)]
+    mods_copy = rdma(mods_0, mods_0, give_send.at[1], give_recv.at[1], sec_dev)
+
+    @pl.when(sec == 0)
+    def _():
+        ada_copy.start()
 
     def build_order():
         lane = lax.broadcasted_iota(jnp.int32, (128, D), 1)
@@ -181,15 +184,14 @@
             natural = lax.broadcasted_iota(jnp.int32, (128, D), 0) + i * 128
             order[i * 128:(i + 1) * 128, :] = jnp.where(natural == source, 1.0, 0.0).astype(BF16)
 
-    x_mine = x.at[:, pl.ds(col * 128, 128)]
-
-    def lat_copy():
-        return rdma(latp, x_mine, pass_send.at[4], pass_recv.at[4], col_dev)
-
-    own_cond.wait()
-    rdma(
-        cond_ref, cbuf.at[z, yy, pl.ds((1 - xh) * 32, 32)], cond_send.at[0], cond_recv.at[0], xh_dev
-    ).wait_recv()
+    def lat_copy(j):
+        return rdma(
+            latp.at[j], x.at[j, pl.ds(col * 128, 128)], pass_send.at[4 + j], pass_recv.at[4 + j], col_dev
+        )
+
+    def send_piece(k):
+        xh_arrival(k).wait_recv()
+        near(k, 0)
 
     def cond_y(d, arrival):
         ref = cbuf.at[z, y_peer[4 - d] if arrival else yy]
@@ -205,62 +207,79 @@
     def part_y(d):
         return rdma(sum_z.at[y_peer[d]], got_y.at[d - 1], sum_send.at[d + 2], sum_recv.at[d + 2], at(y_=y_peer[d]))
 
-    for d in (1, 3, 2):
-        cond_y(d, False).start()
-    for d in (1, 3, 2):
-        cond_y(d, True).wait_recv()
-    for d in (1, 3, 2):
-        cond_z(d, False).start()
-    build_order()
-    for d in (1, 3, 2):
-        cond_z(d, True).wait_recv()
-    for i in range(32):
-        cmat[i:i + 1, :] = cbuf[i // 8, (i // 2) % 4, pl.ds((i % 2) * 32 + row, 1), :]
-    products = jnp.dot(cmat[...].astype(BF16), ada_ref[...], preferred_element_type=F32)
-    for i in range(32):
-        part[i // 8, (i // 2) % 4, i % 2] = products[i:i + 1, :]
-    for d in (1, 3, 2):
-        part_z(d).start()
-
-    @pl.when(sec == 0)
+    part_x = rdma(sum_y.at[1 - xh], got_x, sum_send.at[6], sum_recv.at[6], xh_dev)
+    mod_copy = rdma(mods.at[col], mods.at[col], sum_send.at[7], sum_recv.at[7], col_dev)
+
+    @pl.when(sec == 1)
     def _():
-        for j in range(4):
-            latp[j] = jnp.dot(lat_ref[place_ref[j]], order[...], preferred_element_type=F32).astype(BF16)
-
+        own_cond.start()
+        cond_xh.start()
+        own_cond.wait()
+        rdma(
+            cond_ref, cbuf.at[z, yy, pl.ds((1 - xh) * 32, 32)], cond_send.at[0], cond_recv.at[0], xh_dev
+        ).wait_recv()
+        for d in (1, 3, 2):
+            cond_y(d, False).start()
+        for d in (1, 3, 2):
+            cond_y(d, True).wait_recv()
+        for d in (1, 3, 2):
+            cond_z(d, False).start()
+        for d in (1, 3, 2):
+            cond_z(d, True).wait_recv()
+        for i in range(32):
+            cmat[i:i + 1, :] = cbuf[i // 8, (i // 2) % 4, pl.ds((i % 2) * 32 + row, 1), :]
+        ada_copy.wait_recv()
+        for n, weight in ((0, ada_got), (1, ada_ref)):
+            products = jnp.dot(
+                cmat[:, :ADAROWS].astype(BF16), weight[...], preferred_element_type=F32
+            )
+            for i in range(32):
+                part[i // 8, (i // 2) % 4, i % 2, :, n * MODW:(n + 1) * MODW] = products[i:i + 1, :]
+        for d in (1, 3, 2):
+            part_z(d).start()
+        for d in (1, 3, 2):
+            part_z(d).wait_recv()
+        sum_z[...] = part[z] + got_z[0] + got_z[1] + got_z[2]
+        for d in (1, 3, 2):
+            part_y(d).start()
+        for d in (1, 3, 2):
+            part_y(d).wait_recv()
+        sum_y[...] = sum_z[yy] + got_y[0] + got_y[1] + got_y[2]
+        part_x.start()
+        part_x.wait_recv()
+        mods[col] = sum_y[xh] + got_x[...]
+        mod_copy.start()
+        rdma(
+            mods.at[1 - col], mods.at[1 - col], sum_send.at[7], sum_recv.at[7], col_dev
+        ).wait_recv()
+        mods_copy.start()
+
+    await_go()
+    for k in pieces:
+        xh_copy(k).start()
     own_main.wait()
     own_rem.wait()
     await_go()
     for k in pieces:
-        xh_arrival(k).wait_recv()
-        near(k, 0)
+        send_piece(k)
     go()
-
-    @pl.when(sec == 0)
-    def _():
-        lat_copy().start()
-        x[:, pl.ds(col * 128, 128), :] = latp[...]
-
-    for d in (1, 3, 2):
-        part_z(d).wait_recv()
-    sum_z[...] = part[z] + got_z[0] + got_z[1] + got_z[2]
-    for d in (1, 3, 2):
-        part_y(d).start()
     for k in pieces:
         relay_on(k, 0)
-    for d in (1, 3, 2):
-        part_y(d).wait_recv()
-    sum_y[...] = sum_z[yy] + got_y[0] + got_y[1] + got_y[2]
-    part_x = rdma(sum_y.at[1 - xh], got_x, sum_send.at[6], sum_recv.at[6], xh_dev)
-    part_x.start()
     await_go()
     far_arrived(0, 0)
     near(0, 1)
     far_arrived(1, 0)
     near(1, 1)
-    part_x.wait_recv()
-    mod_own[...] = sum_y[xh] + got_x[...]
-    mod_copy = rdma(mod_own, mod_got, sum_send.at[7], sum_recv.at[7], col_dev)
-    mod_copy.start()
+    build_order()
+
+    @pl.when(sec == 0)
+    def _():
+        for j in range(4):
+            latp[j] = jnp.dot(lat_ref[place_ref[j]], order[...], preferred_element_type=F32).astype(BF16)
+        for j in range(4):
+            lat_copy(j).start()
+        x[:, pl.ds(col * 128, 128), :] = latp[...]
+
     far_arrived(2, 0)
     far_arrived(3, 0)
     relay_on(0, 1)
@@ -276,13 +295,6 @@
         token = lax.broadcasted_iota(jnp.int32, (1, 256), 1) + place_ref[j] * 256
         mask_ref[:, j * 256:(j + 1) * 256] = jnp.where(token < length_ref[0], 0.0, -1e30)
     att[...] = jnp.zeros_like(att)
-
-    mod_copy.wait_recv()
-    for k in range(6):
-        base = k * HEADW
-        mod_ref[k:k + 1, pl.ds(col * 512, 512)] = mod_own[:, base:base + 512]
-        mod_ref[k:k + 1, pl.ds((1 - col) * 512, 512)] = mod_got[:, base:base + 512]
-        mod_ref[k:k + 1, MAIN:] = mod_own[:, base + 512:base + HEADW] + mod_got[:, base + 512:base + HEADW]
 
     relay_on(1, 1)
     near(3, 1)
@@ -344,13 +356,23 @@
         def _():
             act(half_copy(j))
 
-    far_arrived(1, 1)
-
     @pl.when(sec == 0)
     def _():
-        lat_copy().wait_recv()
+        mods_copy.wait_recv()
+    for k in range(6):
+        base = pl.multiple_of(sec * MODW + k * HEADW, 128)
+        rest_base = pl.multiple_of(base + 512, 128)
+        for c in (0, 1):
+            mod_ref[k:k + 1, c * 512:(c + 1) * 512] = mods[c, :, pl.ds(base, 512)]
+        mod_ref[k:k + 1, MAIN:] = mods[0, :, pl.ds(rest_base, 128)] + mods[1, :, pl.ds(rest_base, 128)]
+
+    far_arrived(1, 1)
 
     def attend_step(j):
+        @pl.when(sec == 0)
+        def _():
+            lat_copy(j).wait_recv()
+
         @pl.when(sec == 1)
         def _():
             pass_copy(j).wait_recv()
@@ -425,31 +447,27 @@
             y[j, pl.ds(col * 128, 128), :], order[...], NT, preferred_element_type=F32
         ).astype(BF16)
 
-    def step(t, carry):
-        @pl.when(t < 4)
-        def _():
-            attend_step(t)
+    def first_half(t, carry):
+        attend_step(t)
 
         @pl.when(t == 0)
         def _():
             relay_on(2, 1)
             relay_on(3, 1)
             go()
-
-        @pl.when(t == 1)
-        def _():
-            far_arrived(2, 1)
-            far_arrived(3, 1)
-
-        @pl.when(t > 1)
-        def _():
-            finish(t - 2)
+        return carry
+    lax.fori_loop(0, 4, first_half, 0)
+    far_arrived(2, 1)
+    far_arrived(3, 1)
+
+    def second_half(t, carry):
+        mlp_step(t)
 
         @pl.when(t > 0)
         def _():
-            mlp_step(t - 1)
+            finish(t - 1)
         return carry
-    lax.fori_loop(0, 5, step, 0)
+    lax.fori_loop(0, 4, second_half, 0)
     finish(3)
     for p in range(4):
         slot = jnp.int32(0)
@@ -457,14 +475,22 @@
             slot = jnp.where(place_ref[j] == p, j, slot)
         out_ref[p] = yout[slot]
 
-    cond_xh.wait_send()
-    for d in (1, 2, 3):
-        cond_y(d, False).wait_send()
-        cond_z(d, False).wait_send()
-        part_z(d).wait_send()
-        part_y(d).wait_send()
-    part_x.wait_send()
-    mod_copy.wait_send()
+    @pl.when(sec == 0)
+    def _():
+        ada_copy.wait_send()
+
+    @pl.when(sec == 1)
+    def _():
+        cond_xh.wait_send()
+        for d in (1, 2, 3):
+            cond_y(d, False).wait_send()
+            cond_z(d, False).wait_send()
+            part_z(d).wait_send()
+            part_y(d).wait_send()
+        part_x.wait_send()
+        mod_copy.wait_send()
+        mods_copy.wait_send()
+
     for k in pieces:
         xh_copy(k).wait_send()
         for phase in (0, 1):
@@ -479,12 +505,9 @@
         @pl.when(sec == 0)
         def _():
             pass_copy(j).wait_send()
+            lat_copy(j).wait_send()
         return c
     lax.fori_loop(0, 4, drain, 0)
-
-    @pl.when(sec == 0)
-    def _():
-        lat_copy().wait_send()
 
 
 def run_relay(place, length, cond, ada, lat, stale_k, stale_v, main, rem):
@@ -504,14 +527,14 @@
             pltpu.VMEM((4, 128, D), BF16),
             pltpu.VMEM((4, 4, 64, 128), F32),
             pltpu.VMEM((32, 128), F32),
-            pltpu.VMEM((4, 4, 2, 1, MODW), F32),
-            pltpu.VMEM((3, 4, 2, 1, MODW), F32),
-            pltpu.VMEM((4, 2, 1, MODW), F32),
-            pltpu.VMEM((3, 2, 1, MODW), F32),
-            pltpu.VMEM((2, 1, MODW), F32),
-            pltpu.VMEM((1, MODW), F32),
-            pltpu.VMEM((1, MODW), F32),
-            pltpu.VMEM((1, MODW), F32),
+            pltpu.VMEM((ADAROWS, MODW), BF16),
+            pltpu.VMEM((4, 4, 2, 1, 2 * MODW), F32),
+            pltpu.VMEM((3, 4, 2, 1, 2 * MODW), F32),
+            pltpu.VMEM((4, 2, 1, 2 * MODW), F32),
+            pltpu.VMEM((3, 2, 1, 2 * MODW), F32),
+            pltpu.VMEM((2, 1, 2 * MODW), F32),
+            pltpu.VMEM((1, 2 * MODW), F32),
+            pltpu.VMEM((2, 1, 2 * MODW), F32),
             pltpu.VMEM((8, D), F32),
             pltpu.VMEM((4, 4, 64, COLS), BF16),
             pltpu.VMEM((4, 4, 32, QUARTER), BF16),
@@ -529,6 +552,8 @@
             pltpu.VMEM(tokens, BF16),
             pltpu.VMEM(tokens, BF16),
             pltpu.VMEM(tokens, BF16),
+            pltpu.SemaphoreType.DMA((2,)),
+            pltpu.SemaphoreType.DMA((2,)),
             pltpu.SemaphoreType.DMA((7,)),
             pltpu.SemaphoreType.DMA((7,)),
             pltpu.SemaphoreType.DMA((8,)),
@@ -541,8 +566,8 @@
             pltpu.SemaphoreType.DMA((64,)),
             pltpu.SemaphoreType.DMA((8,)),
             pltpu.SemaphoreType.DMA((8,)),
-            pltpu.SemaphoreType.DMA((5,)),
-            pltpu.SemaphoreType.DMA((5,)),
+            pltpu.SemaphoreType.DMA((8,)),
+            pltpu.SemaphoreType.DMA((8,)),
         ],
         compiler_params=pltpu.CompilerParams(
             collective_id=0, has_side_effects=True, vmem_limit_bytes=67043328
@@ -572,7 +597,7 @@
     )
     spread = (to_col[:, None] == jnp.arange(HEADW, dtype=jnp.int32)[None, :]).astype(BF16)
     ada = jnp.einsum("dkc,ce->dke", ada_weight[0], spread, preferred_element_type=F32).astype(BF16)
-    ada = jnp.pad(ada.reshape(36, MODW), ((0, 92), (0, 0)))
+    ada = jnp.pad(ada.reshape(36, MODW), ((0, ADAROWS - 36), (0, 0)))
 
     pad = lambda a, n: jnp.pad(a, ((0, 0), (0, n - a.shape[1])))
     shard = jnp.concatenate(

time: 209 us -> 183 us (0.88)
  Pallas kernels: 195 us -> 170 us
    pallas_call x1, Pallas kernels: 195 us -> 170 us  [run_relay(): pl.pallas_call(relay, out_shape=jax.ShapeDtypeStruct((4, 128, D), BF16),...]
where the time goes in v5:
time: 183 us
  Pallas kernels  170 us (93%)
  local copies, waits for them, and re-layouts  8.68 us (5%)
    pallas_call x1, Pallas kernels, run_relay(): pl.pallas_call(relay, out_shape=jax.ShapeDtypeStruct((4, 128, D), BF16),...  170 us
    unnamed x20, local copies, waits for them, and re-layouts  5.44 us

profile of v5, /device:TPU:1, one launch (start us, length us, event | category | flops | bytes accessed | tf_op | source)
XLA Modules:
  0.0 182.7 jit_solution(13248587529093099696)
XLA Ops:
  1.3 0.1 fusion.17
  1.4 0.1 maximum_reduce_fusion
  1.5 0.1 concatenate.13
  1.6 0.6 pad_convert_fusion.cond_ref
  2.2 0.9 slice_bitcast_fusion
  3.1 1.6 fusion.6
  4.7 0.0 copy-start.4
  4.7 0.0 copy-start.2
  4.8 0.1 pad.32
  4.8 0.0 copy-start.3
  4.9 0.8 pad.25.ada_ref
  5.7 0.0 copy-start
  5.7 0.0 copy-done.4
  5.7 0.0 copy-done.2
  5.8 0.0 copy-done.3
  5.8 0.8 slice.20.main_ref
  6.6 0.6 reshape.76.rem_ref
  7.3 0.0 copy-done
  7.3 0.0 copy-start.1
  7.3 1.4 copy.17
  8.7 0.0 copy-done.1
  8.7 1.4 copy.18
  10.1 170.2 %shard_map.109 = bf16[4,128,1152]{2,1,0:T(8,128)(2,1)} custom-call(s32[4]{0:T(128)} %place_ref.1, s32[1]{0:T(128)S(6)} %copy.28.length_ref, f32[32,128]{1,0:T(8,128)} %pad_convert_fusion.cond_ref, bf16[48,3840]{1,0:T(8,128)(2,1)} %pad.25.ada_ref, bf16[4,128,1152]{2,1,0:T(8,128)(2,1)} %bitcast.43, bf16[4,256,576]{2,1,0:T(8,128)(2,1)} %bitcast.38, ...), custom_call_target="tpu_custom_call" | custom-call | tf_op jit(solution)/shard_map/pallas_call | solution.py:516
  180.3 2.4 %copy.29 = bf16[1,1,4,128,1152]{4,3,2,1,0:T(8,128)(2,1)} copy(bf16[1,1,4,128,1152]{4,3,2,1,0:T(8,128)(2,1)} %bitcast.40) | data formatting | bytes 2359296
  (11 shorter events, 0.2 us)
Async XLA Ops:
  4.7 1.0 copy-start.4
  4.7 1.0 copy-start.2
  4.8 1.0 copy-start.3
  5.7 1.6 copy-start
  7.3 1.4 copy-start.1

commit v6 on v5

--- a/solution.py
+++ b/solution.py
@@ -167,8 +167,7 @@
     own_keys.start()
     own_values.start()
     ada_copy = rdma(ada_ref, ada_got, give_send.at[0], give_recv.at[0], sec_dev)
-    mods_0 = mods.at[:, :, pl.ds(0, MODW)]
-    mods_copy = rdma(mods_0, mods_0, give_send.at[1], give_recv.at[1], sec_dev)
+    mods_copy = rdma(mods.at[0], mods.at[0], give_send.at[1], give_recv.at[1], sec_dev)
 
     @pl.when(sec == 0)
     def _():
@@ -201,14 +200,20 @@
         ref = cbuf.at[z_peer[4 - d] if arrival else z]
         return rdma(ref, ref, cond_send.at[3 + d], cond_recv.at[3 + d], at(zz=z_peer[d]))
 
-    def part_z(d):
-        return rdma(part.at[z_peer[d]], got_z.at[d - 1], sum_send.at[d - 1], sum_recv.at[d - 1], at(zz=z_peer[d]))
-
-    def part_y(d):
-        return rdma(sum_z.at[y_peer[d]], got_y.at[d - 1], sum_send.at[d + 2], sum_recv.at[d + 2], at(y_=y_peer[d]))
-
-    part_x = rdma(sum_y.at[1 - xh], got_x, sum_send.at[6], sum_recv.at[6], xh_dev)
-    mod_copy = rdma(mods.at[col], mods.at[col], sum_send.at[7], sum_recv.at[7], col_dev)
+    def summing(n, src, dst, i, dev):
+        return rdma(src, dst, sum_send.at[n * 8 + i], sum_recv.at[n * 8 + i], dev)
+
+    def part_z(n, d):
+        return summing(n, part.at[n, z_peer[d]], got_z.at[n, d - 1], d - 1, at(zz=z_peer[d]))
+
+    def part_y(n, d):
+        return summing(n, sum_z.at[n, y_peer[d]], got_y.at[n, d - 1], d + 2, at(y_=y_peer[d]))
+
+    def part_x(n):
+        return summing(n, sum_y.at[n, 1 - xh], got_x.at[n], 6, xh_dev)
+
+    def mod_copy(n, c):
+        return summing(n, mods.at[n, c], mods.at[n, c], 7, col_dev)
 
     @pl.when(sec == 1)
     def _():
@@ -234,56 +239,37 @@
                 cmat[:, :ADAROWS].astype(BF16), weight[...], preferred_element_type=F32
             )
             for i in range(32):
-                part[i // 8, (i // 2) % 4, i % 2, :, n * MODW:(n + 1) * MODW] = products[i:i + 1, :]
-        for d in (1, 3, 2):
-            part_z(d).start()
-        for d in (1, 3, 2):
-            part_z(d).wait_recv()
-        sum_z[...] = part[z] + got_z[0] + got_z[1] + got_z[2]
-        for d in (1, 3, 2):
-            part_y(d).start()
-        for d in (1, 3, 2):
-            part_y(d).wait_recv()
-        sum_y[...] = sum_z[yy] + got_y[0] + got_y[1] + got_y[2]
-        part_x.start()
-        part_x.wait_recv()
-        mods[col] = sum_y[xh] + got_x[...]
-        mod_copy.start()
-        rdma(
-            mods.at[1 - col], mods.at[1 - col], sum_send.at[7], sum_recv.at[7], col_dev
-        ).wait_recv()
-        mods_copy.start()
+                part[n, i // 8, (i // 2) % 4, i % 2] = products[i:i + 1, :]
+            for d in (1, 3, 2):
+                part_z(n, d).start()
+            for d in (1, 3, 2):
+                part_z(n, d).wait_recv()
+            sum_z[n] = part[n, z] + got_z[n, 0] + got_z[n, 1] + got_z[n, 2]
+            for d in (1, 3, 2):
+                part_y(n, d).start()
+            for d in (1, 3, 2):
+                part_y(n, d).wait_recv()
+            sum_y[n] = sum_z[n, yy] + got_y[n, 0] + got_y[n, 1] + got_y[n, 2]
+            part_x(n).start()
+            part_x(n).wait_recv()
+            mods[n, col] = sum_y[n, xh] + got_x[n]
+            mod_copy(n, col).start()
+            mod_copy(n, 1 - col).wait_recv()
+            if n == 0:
+                mods_copy.start()
 
     await_go()
     for k in pieces:
         xh_copy(k).start()
     own_main.wait()
     own_rem.wait()
-    await_go()
-    for k in pieces:
-        send_piece(k)
-    go()
-    for k in pieces:
-        relay_on(k, 0)
-    await_go()
-    far_arrived(0, 0)
-    near(0, 1)
-    far_arrived(1, 0)
-    near(1, 1)
     build_order()
 
     @pl.when(sec == 0)
     def _():
         for j in range(4):
             latp[j] = jnp.dot(lat_ref[place_ref[j]], order[...], preferred_element_type=F32).astype(BF16)
-        for j in range(4):
-            lat_copy(j).start()
         x[:, pl.ds(col * 128, 128), :] = latp[...]
-
-    far_arrived(2, 0)
-    far_arrived(3, 0)
-    relay_on(0, 1)
-    near(2, 1)
 
     own_keys.wait()
     own_values.wait()
@@ -296,9 +282,33 @@
         mask_ref[:, j * 256:(j + 1) * 256] = jnp.where(token < length_ref[0], 0.0, -1e30)
     att[...] = jnp.zeros_like(att)
 
+    await_go()
+    send_piece(0)
+    send_piece(1)
+    relay_on(0, 0)
+    relay_on(1, 0)
+    await_go()
+    far_arrived(0, 0)
+    near(0, 1)
+    far_arrived(1, 0)
+    near(1, 1)
+    send_piece(2)
+    send_piece(3)
+    go()
+
+    @pl.when(sec == 0)
+    def _():
+        for j in range(4):
+            lat_copy(j).start()
+
+    relay_on(2, 0)
+    relay_on(3, 0)
+    relay_on(0, 1)
     relay_on(1, 1)
+    far_arrived(2, 0)
+    near(2, 1)
+    far_arrived(3, 0)
     near(3, 1)
-    go()
     far_arrived(0, 1)
     rows_i = lax.broadcasted_iota(jnp.int32, (128, 512), 0)
     cols_i = lax.broadcasted_iota(jnp.int32, (128, 512), 1)
@@ -360,11 +370,12 @@
     def _():
         mods_copy.wait_recv()
     for k in range(6):
-        base = pl.multiple_of(sec * MODW + k * HEADW, 128)
-        rest_base = pl.multiple_of(base + 512, 128)
+        base = k * HEADW
         for c in (0, 1):
-            mod_ref[k:k + 1, c * 512:(c + 1) * 512] = mods[c, :, pl.ds(base, 512)]
-        mod_ref[k:k + 1, MAIN:] = mods[0, :, pl.ds(rest_base, 128)] + mods[1, :, pl.ds(rest_base, 128)]
+            mod_ref[k:k + 1, c * 512:(c + 1) * 512] = mods[sec, c, :, base:base + 512]
+        mod_ref[k:k + 1, MAIN:] = (
+            mods[sec, 0, :, base + 512:base + HEADW] + mods[sec, 1, :, base + 512:base + HEADW]
+        )
 
     far_arrived(1, 1)
 
@@ -455,6 +466,7 @@
             relay_on(2, 1)
             relay_on(3, 1)
             go()
+            go()
         return carry
     lax.fori_loop(0, 4, first_half, 0)
     far_arrived(2, 1)
@@ -485,10 +497,12 @@
         for d in (1, 2, 3):
             cond_y(d, False).wait_send()
             cond_z(d, False).wait_send()
-            part_z(d).wait_send()
-            part_y(d).wait_send()
-        part_x.wait_send()
-        mod_copy.wait_send()
+            for n in (0, 1):
+                part_z(n, d).wait_send()
+                part_y(n, d).wait_send()
+        for n in (0, 1):
+            part_x(n).wait_send()
+            mod_copy(n, col).wait_send()
         mods_copy.wait_send()
 
     for k in pieces:
@@ -516,7 +530,7 @@
     return pl.pallas_call(
         relay,
         out_shape=jax.ShapeDtypeStruct((4, 128, D), BF16),
-        in_specs=[pl.BlockSpec(memory_space=pltpu.SMEM)] * 2 + [vmem] * 3 + [pl.BlockSpec(memory_space=pl.ANY)] * 2 + [vmem] * 2,
+        in_specs=[pl.BlockSpec(memory_space=pltpu.SMEM)] * 2 + [vmem] * 3 + [pl.BlockSpec(memory_space=pltpu.HBM)] * 2 + [vmem] * 2,
         out_specs=vmem,
         scratch_shapes=[
             pltpu.VMEM((D, D), BF16),
@@ -528,13 +542,13 @@
             pltpu.VMEM((4, 4, 64, 128), F32),
             pltpu.VMEM((32, 128), F32),
             pltpu.VMEM((ADAROWS, MODW), BF16),
-            pltpu.VMEM((4, 4, 2, 1, 2 * MODW), F32),
-            pltpu.VMEM((3, 4, 2, 1, 2 * MODW), F32),
-            pltpu.VMEM((4, 2, 1, 2 * MODW), F32),
-            pltpu.VMEM((3, 2, 1, 2 * MODW), F32),
-            pltpu.VMEM((2, 1, 2 * MODW), F32),
-            pltpu.VMEM((1, 2 * MODW), F32),
-            pltpu.VMEM((2, 1, 2 * MODW), F32),
+            pltpu.VMEM((2, 4, 4, 2, 1, MODW), F32),
+            pltpu.VMEM((2, 3, 4, 2, 1, MODW), F32),
+            pltpu.VMEM((2, 4, 2, 1, MODW), F32),
+            pltpu.VMEM((2, 3, 2, 1, MODW), F32),
+            pltpu.VMEM((2, 2, 1, MODW), F32),
+            pltpu.VMEM((2, 1, MODW), F32),
+            pltpu.VMEM((2, 2, 1, MODW), F32),
             pltpu.VMEM((8, D), F32),
             pltpu.VMEM((4, 4, 64, COLS), BF16),
             pltpu.VMEM((4, 4, 32, QUARTER), BF16),
@@ -556,8 +570,8 @@
             pltpu.SemaphoreType.DMA((2,)),
             pltpu.SemaphoreType.DMA((7,)),
             pltpu.SemaphoreType.DMA((7,)),
-            pltpu.SemaphoreType.DMA((8,)),
-            pltpu.SemaphoreType.DMA((8,)),
+            pltpu.SemaphoreType.DMA((16,)),
+            pltpu.SemaphoreType.DMA((16,)),
             pltpu.SemaphoreType.REGULAR,
             pltpu.SemaphoreType.DMA((5,)),
             pltpu.SemaphoreType.DMA((4,)),

time: 183 us -> 179 us (0.978)
  Pallas kernels: 170 us -> 166 us
    pallas_call x1, Pallas kernels: 170 us -> 166 us  [run_relay(): pl.pallas_call(relay, out_shape=jax.ShapeDtypeStruct((4, 128, D), BF16),...]
where the time goes in v6:
time: 179 us; the launch traced here: 178 us
  Pallas kernels  166 us (93%)
  local copies, waits for them, and re-layouts  8.68 us (5%)
    pallas_call x1, Pallas kernels, run_relay(): pl.pallas_call(relay, out_shape=jax.ShapeDtypeStruct((4, 128, D), BF16),...  166 us
    unnamed x20, local copies, waits for them, and re-layouts  5.44 us

profile of v6, /device:TPU:1, one launch (start us, length us, event | category | flops | bytes accessed | tf_op | source)
XLA Modules:
  0.0 178.4 jit_solution(13063650684851343552)
XLA Ops:
  1.3 0.1 fusion.17
  1.4 0.1 maximum_reduce_fusion
  1.5 0.1 concatenate.13
  1.6 0.6 pad_convert_fusion.cond_ref
  2.2 0.9 slice_bitcast_fusion
  3.1 1.6 fusion.6
  4.7 0.0 copy-start.4
  4.7 0.0 copy-start.2
  4.8 0.1 pad.32
  4.8 0.0 copy-start.3
  4.9 0.8 pad.25.ada_ref
  5.7 0.0 copy-start
  5.7 0.0 copy-done.4
  5.7 0.0 copy-done.2
  5.8 0.0 copy-done.3
  5.8 0.8 slice.20.main_ref
  6.6 0.6 reshape.76.rem_ref
  7.3 0.0 copy-done
  7.3 0.0 copy-start.1
  7.3 1.4 copy.17
  8.7 0.0 copy-done.1
  8.7 1.4 copy.18
  10.1 165.9 %shard_map.109 = bf16[4,128,1152]{2,1,0:T(8,128)(2,1)} custom-call(s32[4]{0:T(128)} %place_ref.1, s32[1]{0:T(128)S(6)} %copy.28.length_ref, f32[32,128]{1,0:T(8,128)} %pad_convert_fusion.cond_ref, bf16[48,3840]{1,0:T(8,128)(2,1)} %pad.25.ada_ref, bf16[4,128,1152]{2,1,0:T(8,128)(2,1)} %bitcast.43, bf16[4,256,576]{2,1,0:T(8,128)(2,1)} %bitcast.38, ...), custom_call_target="tpu_custom_call" | custom-call | tf_op jit(solution)/shard_map/pallas_call | solution.py:530
  176.1 2.4 %copy.29 = bf16[1,1,4,128,1152]{4,3,2,1,0:T(8,128)(2,1)} copy(bf16[1,1,4,128,1152]{4,3,2,1,0:T(8,128)(2,1)} %bitcast.40) | data formatting | bytes 2359296
  (11 shorter events, 0.2 us)
Async XLA Ops:
  4.7 1.0 copy-start.4
  4.7 1.0 copy-start.2
  4.8 1.0 copy-start.3
  5.7 1.6 copy-start
  7.3 1.4 copy-start.1
